TPU v7x, 32 devices: a whole 2x2x4 slice. The times are simulated.
32 devices in a mesh: dp: 8 (over z, x), tensor: 4 (over y, core).
Axes of the slice: x: 2, y: 2, z: 4, core: 2. Of those that a mesh axis runs over, the one named last changes fastest.
Arguments:
- tokens: bfloat16 [1024, 8192], P('dp', 'tensor'), may hold values from -6 to 6
- key_value_weight: bfloat16 [8192, 2048], P('tensor'), may hold values from -0.0625 to 0.0625
- adapter_down_weight: bfloat16 [24, 64, 8192], P('dp', None, 'tensor'), may hold values from -0.0625 to 0.0625
- adapter_up_weight: bfloat16 [24, 64, 2048], P('dp', None, 'tensor'), may hold values from -0.75 to 0.75
- cotangent: bfloat16 [1024, 2048], P('dp', 'tensor'), may hold values from -3 to 3
- sequence_adapter_index: int32 [32], replicated, may hold values from 0 to 23, as said below
- adapter_storage_row: int32 [24], replicated, may hold values from 0 to 23, as said below
Outputs:
- key_value_output: bfloat16 [1024, 2048], P('dp', 'tensor')
- token_gradient: bfloat16 [1024, 8192], P('dp', 'tensor')
- grad_down: float32 [24, 64, 8192], P('dp', None, 'tensor')
- grad_up: float32 [24, 64, 2048], P('dp', None, 'tensor')
Inputs may be any that keep to these rules, and one draw needn't show every extreme that they name: Each value appears once: adapter a is held at row adapter_storage_row[a] of adapter_down_weight, adapter_up_weight, grad_down and grad_up, on index adapter_storage_row[a] // 3 of dp. `sequence_adapter_index`: the 4 sequences i that share one value of i // 4 use adapters held on 4 different indices of dp.
All inputs are finite; a program needn't handle non-finite values.
Results may differ from a plain program's by a relative error of at most 0.02.
Values may be sent and summed in bfloat16 or wider, within the bound.
A program may use at most 64 MiB of HBM per device.

v0:
```python
import functools

import jax
import jax.numpy as jnp
from jax import lax
from jax.experimental import pallas as pl
from jax.experimental.pallas import tpu as pltpu
from jax.sharding import PartitionSpec as P

adapter_scale = 0.25
MESH = pl.DeviceIdType.MESH
F32 = jnp.float32
BF16 = jnp.bfloat16


def nt_dot(a, b):
    return lax.dot_general(a, b, (((1,), (1,)), ((), ())), preferred_element_type=F32)


def tn_dot(a, b):
    return lax.dot_general(a, b, (((0,), (0,)), ((), ())), preferred_element_type=F32)


def partner(d, k, dp_count):
    out, bit = d, 1
    while bit < dp_count:
        if k & bit:
            out = out + bit - 2 * bit * lax.rem(lax.div(d, jnp.int32(bit)), jnp.int32(2))
        bit *= 2
    return out


def routes(dp_count, seqs, resident, seq_ref, store_ref, table_ref, weight_ref):
    d = lax.axis_index("dp")
    rows = [store_ref[seq_ref[d * seqs + j]] for j in range(seqs)]
    owners = [lax.div(r, jnp.int32(resident)) for r in rows]
    dist = []
    for j in range(seqs):
        slot = jnp.int32(0)
        for k in range(1, dp_count):
            slot = jnp.where(owners[j] == partner(d, k, dp_count), jnp.int32(k), slot)
        dist.append(slot)
    for j in range(seqs):
        table_ref[2 * dp_count + j] = dist[j]
    for k in range(dp_count):
        pick = jnp.int32(0)
        for j in range(seqs):
            pick = jnp.where(dist[j] == k, jnp.int32(j), pick)
        table_ref[k] = pick
    counts = [jnp.float32(0.0)] * resident
    for k in range(dp_count):
        reader = partner(d, k, dp_count)
        found = jnp.int32(-1)
        for j in range(seqs):
            local = store_ref[seq_ref[reader * seqs + j]] - d * resident
            found = jnp.where((local >= 0) & (local < resident), local, found)
        table_ref[dp_count + k] = jnp.maximum(found, 0)
        for a in range(resident):
            hit = jnp.where(found == a, jnp.float32(1.0), jnp.float32(0.0))
            weight_ref[a * dp_count + k] = hit
            counts[a] = counts[a] + hit
    for a in range(resident):
        weight_ref[resident * dp_count + a] = counts[a]


def slot_groups(dp_count):
    order = list(range(dp_count - 1, -1, -1))
    quarter = dp_count // 4
    return [order[:quarter], order[quarter:2 * quarter], order[2 * quarter:]]


def kernel(
    dp_count,
    tensor_count,
    table_ref,
    weight_ref,
    tok_ref,
    w_ref,
    down_hbm,
    up_hbm,
    cot_ref,
    cot_seq_ref,
    kvo_ref,
    tg_ref,
    gd_hbm,
    gu_hbm,
    down_ref,
    up_ref,
    gd_ref,
    gu_ref,
    w_v,
    slot_out,
    slot_in,
    ret_out,
    ret_in,
    cots,
    parts,
    part_in,
    ranks,
    back_m,
    inner_m,
    acc,
    w_sem,
    local_sem,
    slot_ssem,
    slot_rsem,
    ret_ssem,
    ret_rsem,
    cot_ssem,
    cot_rsem,
    part_ssem,
    part_rsem,
    rank_ssem,
    rank_rsem,
):
    d = lax.axis_index("dp")
    t = lax.axis_index("tensor")
    resident, rank, block = down_ref.shape
    out_block = up_ref.shape[2]
    seqs, length = tok_ref.shape[:2]
    rows = seqs * length
    groups = slot_groups(dp_count)
    starts = [sum(len(g) for g in groups[:i]) for i in range(len(groups))]

    def dp_to(k):
        return partner(d, k, dp_count)

    def t_to(q):
        return lax.rem(t + q, tensor_count)

    def t_from(q):
        return lax.rem(t + tensor_count - q, tensor_count)

    def w_copy(i):
        c = t_to(i)
        return pltpu.make_async_copy(
            w_ref.at[:, pl.ds(pl.multiple_of(c * out_block, out_block), out_block)],
            w_v.at[i],
            w_sem.at[i],
        )

    down_copy = pltpu.make_async_copy(down_hbm, down_ref, local_sem.at[0])
    up_copy = pltpu.make_async_copy(up_hbm, up_ref, local_sem.at[1])
    gd_copy = pltpu.make_async_copy(gd_ref, gd_hbm, local_sem.at[2])
    gu_copy = pltpu.make_async_copy(gu_ref, gu_hbm, local_sem.at[3])
    for i in range(tensor_count):
        w_copy(i).start()
    down_copy.start()
    up_copy.start()

    barrier = pltpu.get_barrier_semaphore()
    for k in range(1, dp_count):
        pl.semaphore_signal(barrier, inc=1, device_id={"dp": dp_to(k)}, device_id_type=MESH)
    for q in range(1, tensor_count):
        pl.semaphore_signal(barrier, inc=1, device_id={"tensor": t_to(q)}, device_id_type=MESH)

    for k in range(dp_count):
        pick = table_ref[k]
        target = slot_in if k == 0 else slot_out
        target[k * length:(k + 1) * length, :block] = tok_ref[pick]
        target[k * length:(k + 1) * length, block:] = cot_seq_ref[pick]

    pl.semaphore_wait(barrier, dp_count + tensor_count - 2)

    def cot_copy(q):
        return pltpu.make_async_remote_copy(
            cot_ref, cots.at[q], cot_ssem.at[q], cot_rsem.at[q],
            device_id={"tensor": t_to(q)}, device_id_type=MESH)

    def slot_copy(k):
        at = pl.ds(k * length, length)
        return pltpu.make_async_remote_copy(
            slot_out.at[at], slot_in.at[at], slot_ssem.at[k], slot_rsem.at[k],
            device_id={"dp": dp_to(k)}, device_id_type=MESH)

    def ret_copy(k):
        return pltpu.make_async_remote_copy(
            ret_out.at[k], ret_in.at[k], ret_ssem.at[k], ret_rsem.at[k],
            device_id={"dp": dp_to(k)}, device_id_type=MESH)

    def part_copy(q):
        return pltpu.make_async_remote_copy(
            parts.at[q], part_in.at[q], part_ssem.at[q], part_rsem.at[q],
            device_id={"tensor": t_to(q)}, device_id_type=MESH)

    def rank_rows(g):
        return pl.ds(starts[g] * length, len(groups[g]) * length)

    def rank_copy(g, q):
        return pltpu.make_async_remote_copy(
            ranks.at[t, rank_rows(g)], ranks.at[t, rank_rows(g)], rank_ssem.at[g, q], rank_rsem.at[g, q],
            device_id={"tensor": t_to(q)}, device_id_type=MESH)

    for k in range(dp_count - 1, 0, -1):
        slot_copy(k).start()
    for q in range(1, tensor_count):
        cot_copy(q).start()

    adapter_of = [table_ref[dp_count + k] for k in range(dp_count)]
    weights = [[weight_ref[a * dp_count + k] for k in range(dp_count)] for a in range(resident)]
    counts = [weight_ref[resident * dp_count + a] for a in range(resident)]

    def frozen_block(i, carry):
        w_copy(i).wait()
        parts[i] = jnp.dot(tok_ref[...].reshape(rows, block), w_v[i], preferred_element_type=F32).astype(BF16)
        return carry

    lax.fori_loop(0, tensor_count, frozen_block, 0)

    def rank_stage(g):
        for m, k in enumerate(groups[g]):
            if k:
                slot_copy(k).wait_recv()
            x = slot_in[k * length:(k + 1) * length, :block]
            c = slot_in[k * length:(k + 1) * length, block:]
            inner = nt_dot(x, down_ref[adapter_of[k]])
            back = nt_dot(c, up_ref[adapter_of[k]])
            ranks[t, (starts[g] + m) * length:(starts[g] + m + 1) * length, :] = jnp.concatenate(
                [inner, back], axis=1).astype(BF16)
        for q in range(1, tensor_count):
            rank_copy(g, q).start()

    def base_block(i, carry):
        q = lax.rem(tensor_count - i, tensor_count)
        acc[...] += nt_dot(cots[q], w_v[i])
        return carry

    def use_stage(g):
        for q in range(1, tensor_count):
            s = t_from(q)
            pltpu.make_async_remote_copy(
                ranks.at[s, rank_rows(g)], ranks.at[s, rank_rows(g)], rank_ssem.at[g, q], rank_rsem.at[g, q],
                device_id={"tensor": t_to(q)}, device_id_type=MESH).wait_recv()
        for q in range(1, tensor_count):
            rank_copy(g, q).wait_send()
        total = ranks[0, rank_rows(g)].astype(F32)
        for s in range(1, tensor_count):
            total = total + ranks[s, rank_rows(g)].astype(F32)
        for m, k in enumerate(groups[g]):
            lines = total[m * length:(m + 1) * length]
            inner = lines[:, :rank].astype(BF16)
            back = lines[:, rank:].astype(BF16)
            target = ret_out if k else ret_in
            target[k, :, :block] = (adapter_scale * jnp.dot(
                back, down_ref[adapter_of[k]], preferred_element_type=F32)).astype(BF16)
            target[k, :, block:] = (adapter_scale * jnp.dot(
                inner, up_ref[adapter_of[k]], preferred_element_type=F32)).astype(BF16)
            for a in range(resident):
                at = slice(k * length, (k + 1) * length)
                back_m[a, at, :] = (back.astype(F32) * weights[a][k]).astype(BF16)
                inner_m[a, at, :] = (inner.astype(F32) * weights[a][k]).astype(BF16)
            if k:
                ret_copy(k).start()

    for q in range(1, tensor_count):
        part_copy(q).start()
    half = max(1, tensor_count // 2)
    acc[...] = nt_dot(cot_ref[...], w_v[0])
    for q in range(1, tensor_count):
        cot_copy(q).wait_recv()
    lax.fori_loop(1, half, base_block, 0)
    down_copy.wait()
    up_copy.wait()
    rank_stage(0)
    lax.fori_loop(half, tensor_count, base_block, 0)
    use_stage(0)
    rank_stage(1)
    use_stage(1)
    rank_stage(2)
    use_stage(2)

    x_all = slot_in[:, :block]
    c_all = slot_in[:, block:]
    for a in range(resident):
        gd_ref[a] = tn_dot(back_m[a], x_all) * (
            adapter_scale / jnp.maximum(jnp.full((1, block), counts[a], F32), 1.0))
        gu_ref[a] = tn_dot(inner_m[a], c_all) * (
            adapter_scale / jnp.maximum(jnp.full((1, out_block), counts[a], F32), 1.0))

    gd_copy.start()
    gu_copy.start()
    for q in range(1, tensor_count):
        part_copy(q).wait_recv()
    backbone = parts[0].astype(F32)
    for q in range(1, tensor_count):
        backbone = backbone + part_in[q].astype(F32)
    for k in range(1, dp_count):
        ret_copy(k).wait_recv()
    for j in range(seqs):
        at = slice(j * length, (j + 1) * length)
        came = ret_in[table_ref[2 * dp_count + j]]
        kvo_ref[at, :] = (backbone[at] + came[:, block:].astype(F32)).astype(BF16)
        tg_ref[at, :] = (acc[at, :] + came[:, :block].astype(F32)).astype(BF16)

    for k in range(1, dp_count):
        slot_copy(k).wait_send()
        ret_copy(k).wait_send()
    for q in range(1, tensor_count):
        cot_copy(q).wait_send()
        part_copy(q).wait_send()
    gd_copy.wait()
    gu_copy.wait()


def finish(pieces, *refs):
    n = len(pieces)
    given, out, held = refs[:n], refs[n:2 * n], refs[2 * n:3 * n]
    in_sem, out_sem = refs[3 * n:]
    steps = [(i, p) for i in range(n) for p in range(pieces[i])]

    def move(i, p, source, target, sem, at):
        span = source.shape[0] // pieces[i]
        rows = pl.ds(p * span, span)
        return pltpu.make_async_copy(source.at[rows], target.at[rows], sem.at[at])

    for at, (i, p) in enumerate(steps):
        move(i, p, given[i], held[i], in_sem, at).start()
    for at, (i, p) in enumerate(steps):
        move(i, p, given[i], held[i], in_sem, at).wait()
        move(i, p, held[i], out[i], out_sem, at).start()
    for at, (i, p) in enumerate(steps):
        move(i, p, held[i], out[i], out_sem, at).wait()


def on_device(dp_count, tensor_count, tok, w, down, up, cot, seq_index, storage):
    resident, rank, block = down.shape
    out_block = up.shape[2]
    rows = tok.shape[0]
    seqs = seq_index.shape[0] // dp_count
    length = rows // seqs
    groups = len(slot_groups(dp_count))
    anywhere = pl.BlockSpec(memory_space=pl.ANY)
    wide = block + out_block
    vmem = pl.BlockSpec(memory_space=pltpu.VMEM)
    smem = pl.BlockSpec(memory_space=pltpu.SMEM)
    dma = pltpu.SemaphoreType.DMA
    table, weights = pl.pallas_call(
        functools.partial(routes, dp_count, seqs, resident),
        out_shape=(
            jax.ShapeDtypeStruct((2 * dp_count + seqs,), jnp.int32),
            jax.ShapeDtypeStruct((resident * dp_count + resident,), F32),
        ),
        in_specs=[smem, smem],
        out_specs=(smem, smem),
    )(seq_index, storage)
    results = pl.pallas_call(
        functools.partial(kernel, dp_count, tensor_count),
        out_shape=(
            jax.ShapeDtypeStruct((rows, out_block), BF16),
            jax.ShapeDtypeStruct((rows, block), BF16),
            jax.ShapeDtypeStruct((resident, rank, block), F32),
            jax.ShapeDtypeStruct((resident, rank, out_block), F32),
        ),
        in_specs=[smem, smem, vmem, anywhere, anywhere, anywhere, vmem, vmem],
        out_specs=(vmem, vmem, anywhere, anywhere),
        scratch_shapes=[
            pltpu.VMEM(down.shape, BF16),
            pltpu.VMEM(up.shape, BF16),
            pltpu.VMEM(down.shape, F32),
            pltpu.VMEM(up.shape, F32),
            pltpu.VMEM((tensor_count, w.shape[0], out_block), BF16),
            pltpu.VMEM((dp_count * length, wide), BF16),
            pltpu.VMEM((dp_count * length, wide), BF16),
            pltpu.VMEM((dp_count, length, wide), BF16),
            pltpu.VMEM((dp_count, length, wide), BF16),
            pltpu.VMEM((tensor_count, rows, out_block), BF16),
            pltpu.VMEM((tensor_count, rows, out_block), BF16),
            pltpu.VMEM((tensor_count, rows, out_block), BF16),
            pltpu.VMEM((tensor_count, dp_count * length, 2 * rank), BF16),
            pltpu.VMEM((resident, dp_count * length, rank), BF16),
            pltpu.VMEM((resident, dp_count * length, rank), BF16),
            pltpu.VMEM((rows, block), F32),
            dma((tensor_count,)),
            dma((4,)),
            dma((dp_count,)),
            dma((dp_count,)),
            dma((dp_count,)),
            dma((dp_count,)),
            dma((tensor_count,)),
            dma((tensor_count,)),
            dma((tensor_count,)),
            dma((tensor_count,)),
            dma((groups, tensor_count)),
            dma((groups, tensor_count)),
        ],
        compiler_params=pltpu.CompilerParams(
            collective_id=0, has_side_effects=True, vmem_limit_bytes=60 * 1024 * 1024
        ),
    )(
        table, weights, tok.reshape(seqs, length, block), w, down, up, cot,
        cot.reshape(seqs, length, out_block))
    pieces = (1, 2, resident, 1)
    return pl.pallas_call(
        functools.partial(finish, pieces),
        out_shape=tuple(jax.ShapeDtypeStruct(r.shape, r.dtype) for r in results),
        in_specs=[anywhere] * 4,
        out_specs=(anywhere,) * 4,
        scratch_shapes=[pltpu.VMEM(r.shape, r.dtype) for r in results] + [
            dma((sum(pieces),)), dma((sum(pieces),))],
    )(*results)


def solution(mesh):
    in_specs = (
        P("dp", "tensor"),
        P("tensor", None),
        P("dp", None, "tensor"),
        P("dp", None, "tensor"),
        P("dp", "tensor"),
        P(),
        P(),
    )
    out_specs = (
        P("dp", "tensor"),
        P("dp", "tensor"),
        P("dp", None, "tensor"),
        P("dp", None, "tensor"),
    )
    return jax.shard_map(
        functools.partial(on_device, mesh.shape["dp"], mesh.shape["tensor"]),
        mesh=mesh, in_specs=in_specs, out_specs=out_specs, check_vma=False,
    )
```

profile of v0, /device:TPU:0, one launch (start us, length us, event | category | flops | bytes accessed | tf_op | source)
XLA Modules:
  0.0 71.0 jit_solution(13335015475758364166)
XLA Ops:
  0.6 1.4 %shard_map.102 = (s32[20]{0:T(128)}, f32[27]{0:T(128)}) custom-call(s32[32]{0:T(128)} %seq_ref.1, s32[24]{0:T(128)} %store_ref.1), custom_call_target="tpu_custom_call" | custom-call | tf_op jit(solution)/shard_map/pallas_call | solution.py:337
  2.0 66.3 %shard_map.103 = (bf16[128,512]{1,0:T(8,128)(2,1)}, bf16[128,2048]{1,0:T(8,128)(2,1)}, f32[3,64,2048]{2,1,0:T(8,128)}, f32[3,64,512]{2,1,0:T(8,128)}) custom-call(s32[20]{0:T(128)} %get-tuple-element.10.table_ref, f32[27]{0:T(128)} %get-tuple-element.11.weight_ref, bf16[4,32,2048]{2,1,0:T(8,128)(2,1)} %bitcast.3, bf16[2048,2048]{1,0:T(8,128)(2,1)} %w_ref.1, ...), custom_call_target="tpu_custom_call" | custom-call | tf_op jit(solution)/shard_map/pallas_call | solution.py:346
  68.3 2.7 %shard_map.104 = (bf16[128,512]{1,0:T(8,128)(2,1)}, bf16[128,2048]{1,0:T(8,128)(2,1)}, f32[3,64,2048]{2,1,0:T(8,128)}, f32[3,64,512]{2,1,0:T(8,128)}) custom-call(bf16[128,512]{1,0:T(8,128)(2,1)} %get-tuple-element.12.refs_0_, bf16[128,2048]{1,0:T(8,128)(2,1)} %get-tuple-element.13.refs_1_, f32[3,64,2048]{2,1,0:T(8,128)} %get-tuple-element.14.refs_2_, ...), custom_call_target="tpu_custom_call" | custom-call | tf_op jit(solution)/shard_map/pallas_call | solution.py:393
where the time goes:
time: 71.2 us; the launch traced here: 71 us
  Pallas kernels  70.3 us (99%)
    pallas_call x1, Pallas kernels, on_device(): pl.pallas_call(functools.partial(kernel, dp_count, tensor_count), out_sha...  66.3 us
    pallas_call x1, Pallas kernels, on_device(): pl.pallas_call(functools.partial(finish, pieces), out_shape=tuple((jax.Sh...  2.66 us

commit v1 on v0

--- a/solution.py
+++ b/solution.py
@@ -302,6 +302,436 @@
     gu_copy.wait()
 
 
+def mix(first, second, flag):
+    return jnp.where(flag > 0, first, second)
+
+
+def relay_fits(dp_count, seqs):
+    return dp_count == 2 * seqs and seqs == 4
+
+
+def relay_routes(dp_count, seqs, resident, seq_ref, store_ref, table_ref, weight_ref):
+    d = lax.axis_index("dp")
+    half = dp_count // 2
+    xor = lax.bitwise_xor
+    level = lax.div(d, jnp.int32(2))
+    inner = lax.rem(lax.div(level + 1, jnp.int32(2)), jnp.int32(2))
+    home = (2 - lax.div(d, jnp.int32(half))) * 2 + lax.rem(d, jnp.int32(2))
+    zero, one = jnp.int32(0), jnp.int32(1)
+    worst = zero
+    counts = [jnp.float32(0.0)] * resident
+    for k in range(dp_count):
+        p = xor(d, jnp.int32(k))
+        crossing, found = zero, jnp.int32(-1)
+        near = [zero] * half
+        has, which = [zero] * half, [zero] * half
+        apart = []
+        for j in range(seqs):
+            row = store_ref[seq_ref[p * seqs + j]]
+            owner = lax.div(row, jnp.int32(resident))
+            away = xor(owner, p)
+            crossing = crossing + jnp.where(away >= half, one, zero)
+            found = jnp.where(owner == d, row - d * resident, found)
+            if k == 0:
+                step = xor(owner, home)
+                apart.append((away, step))
+                for m in range(half):
+                    near[m] = jnp.where(away == m, jnp.int32(j), near[m])
+            if k in (0, half, half + 2):
+                step = xor(owner, home if k == 0 else d)
+                for m in range(half):
+                    hit = step == half - 1 - m
+                    has[m] = jnp.where(hit, one, has[m])
+                    which[m] = jnp.where(hit, jnp.int32(j), which[m])
+        worst = jnp.maximum(worst, crossing)
+        if k == 0:
+            for m in range(half):
+                table_ref[m] = near[m]
+            table_ref[half] = jnp.where(has[0] > 0, which[0], which[1])
+            table_ref[half + 1] = jnp.where((has[0] > 0) & (has[1] > 0), which[1], which[2])
+            table_ref[half + 2] = jnp.where(has[3] > 0, which[3], which[2])
+            place = [zero, jnp.where(has[0] > 0, one, zero), jnp.where(has[3] > 0, one, jnp.int32(2)), jnp.int32(2)]
+            for j in range(seqs):
+                away, step = apart[j]
+                came = away
+                for m in range(half):
+                    came = jnp.where(step == half - 1 - m, half + place[m], came)
+                table_ref[8 + j] = came
+        if k in (half, half + 2):
+            q = 1 if k == half else 0
+            table_ref[20 + 3 * q] = has[0]
+            table_ref[21 + 3 * q] = has[0] * has[1]
+            table_ref[22 + 3 * q] = has[3]
+        s = jnp.int32(k) if k < half else xor(jnp.int32(k), 2 * inner)
+        table_ref[12 + s] = jnp.maximum(found, 0)
+        for a in range(resident):
+            hit = jnp.where(found == a, jnp.float32(1.0), jnp.float32(0.0))
+            weight_ref[a * dp_count + s] = hit
+            counts[a] = counts[a] + hit
+    for a in range(resident):
+        weight_ref[resident * dp_count + a] = counts[a]
+    table_ref[7] = jnp.where(worst < half, one, zero)
+
+
+def relay_kernel(
+    dp_count,
+    tensor_count,
+    table_ref,
+    weight_ref,
+    tok_ref,
+    w_ref,
+    down_hbm,
+    up_hbm,
+    cot_ref,
+    cot_seq_ref,
+    kvo_ref,
+    tg_ref,
+    gd_hbm,
+    gu_hbm,
+    down_ref,
+    up_ref,
+    gd_ref,
+    gu_ref,
+    w_v,
+    near_out,
+    cross_out,
+    slot_in,
+    relay_in,
+    relay_out,
+    ret_out,
+    ret_in,
+    relay_ret,
+    back_out,
+    cots,
+    parts,
+    part_in,
+    ranks,
+    back_m,
+    inner_m,
+    acc,
+    w_sem,
+    local_sem,
+    near_ssem,
+    slot_rsem,
+    cross_ssem,
+    relay_rsem,
+    fwd_ssem,
+    ret_ssem,
+    ret_rsem,
+    owner_rsem,
+    back_ssem,
+    cot_ssem,
+    cot_rsem,
+    part_ssem,
+    part_rsem,
+    rank_ssem,
+    rank_rsem,
+):
+    d = lax.axis_index("dp")
+    t = lax.axis_index("tensor")
+    resident, rank, block = down_ref.shape
+    out_block = up_ref.shape[2]
+    seqs, length = tok_ref.shape[:2]
+    rows = seqs * length
+    half = dp_count // 2
+    level = lax.div(d, jnp.int32(2))
+    inner = lax.rem(lax.div(level + 1, jnp.int32(2)), jnp.int32(2))
+    outer = 1 - inner
+    home = (2 - lax.div(d, jnp.int32(half))) * 2 + lax.rem(d, jnp.int32(2))
+    peer = [partner(d, k, dp_count) for k in range(dp_count)]
+    groups = [[0, 1, 2, 3], [4, 5], [6, 7]]
+    starts = [0, 4, 6]
+
+    def t_to(q):
+        return lax.rem(t + q, tensor_count)
+
+    def t_from(q):
+        return lax.rem(t + tensor_count - q, tensor_count)
+
+    def lines(s):
+        return slice(s * length, (s + 1) * length)
+
+    def w_copy(i):
+        c = t_to(i)
+        return pltpu.make_async_copy(
+            w_ref.at[:, pl.ds(pl.multiple_of(c * out_block, out_block), out_block)],
+            w_v.at[i],
+            w_sem.at[i],
+        )
+
+    def over(source, target, ssem, rsem, **where):
+        return pltpu.make_async_remote_copy(
+            source, target, ssem, rsem, device_id=where, device_id_type=MESH)
+
+    def slot_at(s):
+        return slot_in.at[pl.ds(s * length, length)]
+
+    def near_copy(k):
+        return over(near_out.at[k - 1], slot_at(k), near_ssem.at[k], slot_rsem.at[k], dp=peer[k])
+
+    def cross_copy(i):
+        return over(cross_out.at[i], relay_in.at[outer, i], cross_ssem.at[i], relay_rsem.at[outer, i], dp=home)
+
+    def cross_came(q, i):
+        return over(cross_out.at[i], relay_in.at[q, i], cross_ssem.at[i], relay_rsem.at[q, i], dp=home)
+
+    def fwd_copy(q, m):
+        source = relay_in.at[q, 0] if m == 0 else relay_out.at[q, m - 1]
+        s = half + 2 * q + (0 if m == 1 else 1)
+        return over(source, slot_at(s), fwd_ssem.at[q, m], slot_rsem.at[s], dp=peer[3 - m])
+
+    def slot_came(s):
+        return over(near_out.at[0], slot_at(s), near_ssem.at[0], slot_rsem.at[s], dp=peer[1])
+
+    def ret_near(k):
+        return over(ret_out.at[k], ret_in.at[k], ret_ssem.at[k], ret_rsem.at[k], dp=peer[k])
+
+    def ret_same(q):
+        s = half + 2 * q
+        return over(ret_out.at[s], relay_ret.at[q, 1], ret_ssem.at[s], owner_rsem.at[q, 1], dp=peer[2])
+
+    def ret_other(q):
+        s = half + 2 * q + 1
+        m = 2 * inner
+        return over(ret_out.at[s], relay_ret.at[q, m], ret_ssem.at[s], owner_rsem.at[q, m],
+                    dp=inner * peer[1] + outer * peer[3])
+
+    def owner_came(q, m):
+        return over(ret_out.at[1], relay_ret.at[q, m], ret_ssem.at[1], owner_rsem.at[q, m], dp=peer[1])
+
+    def back_copy(q, i):
+        return over(back_out.at[q, i], ret_in.at[half + i], back_ssem.at[q, i], ret_rsem.at[half + i],
+                    dp=peer[half + 2 - 2 * q])
+
+    def ret_came(i):
+        return over(ret_out.at[1], ret_in.at[i], ret_ssem.at[1], ret_rsem.at[i], dp=peer[1])
+
+    def cot_copy(q):
+        return over(cot_ref, cots.at[q], cot_ssem.at[q], cot_rsem.at[q], tensor=t_to(q))
+
+    def part_copy(q):
+        return over(parts.at[q], part_in.at[q], part_ssem.at[q], part_rsem.at[q], tensor=t_to(q))
+
+    def rank_rows(g):
+        return pl.ds(starts[g] * length, len(groups[g]) * length)
+
+    def rank_copy(g, q):
+        at = ranks.at[t, rank_rows(g)]
+        return over(at, at, rank_ssem.at[g, q], rank_rsem.at[g, q], tensor=t_to(q))
+
+    def rank_came(g, q):
+        at = ranks.at[t_from(q), rank_rows(g)]
+        return over(at, at, rank_ssem.at[g, q], rank_rsem.at[g, q], tensor=t_to(q))
+
+    down_copy = pltpu.make_async_copy(down_hbm, down_ref, local_sem.at[0])
+    up_copy = pltpu.make_async_copy(up_hbm, up_ref, local_sem.at[1])
+    gd_copy = pltpu.make_async_copy(gd_ref, gd_hbm, local_sem.at[2])
+    gu_copy = pltpu.make_async_copy(gu_ref, gu_hbm, local_sem.at[3])
+
+    barrier = pltpu.get_barrier_semaphore()
+    for k in range(1, dp_count):
+        pl.semaphore_signal(barrier, inc=1, device_id={"dp": peer[k]}, device_id_type=MESH)
+    for q in range(1, tensor_count):
+        pl.semaphore_signal(barrier, inc=1, device_id={"tensor": t_to(q)}, device_id_type=MESH)
+    for i in range(tensor_count):
+        w_copy(i).start()
+    down_copy.start()
+    up_copy.start()
+
+    for i in range(half - 1):
+        pick = table_ref[half + i]
+        cross_out[i, :, :block] = tok_ref[pick]
+        cross_out[i, :, block:] = cot_seq_ref[pick]
+    for k in range(half):
+        pick = table_ref[k]
+        if k == 0:
+            slot_in[:length, :block] = tok_ref[pick]
+            slot_in[:length, block:] = cot_seq_ref[pick]
+        else:
+            near_out[k - 1, :, :block] = tok_ref[pick]
+            near_out[k - 1, :, block:] = cot_seq_ref[pick]
+
+    pl.semaphore_wait(barrier, dp_count + tensor_count - 2)
+
+    @pl.when(inner == 1)
+    def _():
+        for i in range(half - 1):
+            cross_copy(i).start()
+        for k in (3, 2, 1):
+            near_copy(k).start()
+
+    @pl.when(inner == 0)
+    def _():
+        for k in (3, 2, 1):
+            near_copy(k).start()
+        for i in range(half - 1):
+            cross_copy(i).start()
+
+    for q in range(1, tensor_count):
+        cot_copy(q).start()
+
+    adapter_of = [table_ref[12 + s] for s in range(dp_count)]
+    flags = [[table_ref[20 + 3 * q + i] for i in range(3)] for q in range(2)]
+    weights = [[weight_ref[a * dp_count + s] for s in range(dp_count)] for a in range(resident)]
+    counts = [weight_ref[resident * dp_count + a] for a in range(resident)]
+
+    def relay(q, i):
+        @pl.when(inner == 1)
+        def _():
+            cross_came(q, i).wait_recv()
+            if i == 0:
+                fwd_copy(q, 0).start()
+            if i == 1:
+                relay_out[q, 0] = mix(relay_in[q, 1], relay_in[q, 0], flags[q][0])
+                fwd_copy(q, 1).start()
+            if i == 2:
+                relay_out[q, 1] = mix(relay_in[q, 1], relay_in[q, 2], flags[q][2])
+                fwd_copy(q, 2).start()
+                slot_in[lines(half + 2 * q), :] = relay_in[q, 2]
+
+    def hand_back(q):
+        @pl.when(inner == 1)
+        def _():
+            owner_came(q, 0).wait_recv()
+            owner_came(q, 1).wait_recv()
+            back_out[q, 0] = mix(relay_ret[q, 0], relay_ret[q, 1], flags[q][0])
+            back_copy(q, 0).start()
+            owner_came(q, 2).wait_recv()
+            back_out[q, 1] = mix(relay_ret[q, 1], relay_ret[q, 2], flags[q][1])
+            back_copy(q, 1).start()
+            back_out[q, 2] = mix(ret_out[half + 2 * q], relay_ret[q, 2], flags[q][2])
+            back_copy(q, 2).start()
+
+    def frozen_block(i, carry):
+        w_copy(i).wait()
+        parts[i] = jnp.dot(tok_ref[...].reshape(rows, block), w_v[i], preferred_element_type=F32).astype(BF16)
+        return carry
+
+    def base_block(i, carry):
+        q = lax.rem(tensor_count - i, tensor_count)
+        acc[...] += nt_dot(cots[q], w_v[i])
+        return carry
+
+    def rank_stage(g):
+        for s in groups[g]:
+            if s and s < half:
+                slot_came(s).wait_recv()
+            if s >= half and s % 2 == 1:
+                slot_came(s).wait_recv()
+            if s >= half and s % 2 == 0:
+                @pl.when(inner == 0)
+                def _():
+                    slot_came(s).wait_recv()
+        for s in groups[g]:
+            x = slot_in[lines(s), :block]
+            c = slot_in[lines(s), block:]
+            inner_s = nt_dot(x, down_ref[adapter_of[s]])
+            back_s = nt_dot(c, up_ref[adapter_of[s]])
+            ranks[t, lines(s), :] = jnp.concatenate([inner_s, back_s], axis=1).astype(BF16)
+        for q in range(1, tensor_count):
+            rank_copy(g, q).start()
+
+    def use_stage(g):
+        for q in range(1, tensor_count):
+            rank_came(g, q).wait_recv()
+        for q in range(1, tensor_count):
+            rank_copy(g, q).wait_send()
+        total = ranks[0, rank_rows(g)].astype(F32)
+        for s in range(1, tensor_count):
+            total = total + ranks[s, rank_rows(g)].astype(F32)
+        for m, s in enumerate(groups[g]):
+            part = total[m * length:(m + 1) * length]
+            mid = part[:, :rank].astype(BF16)
+            back = part[:, rank:].astype(BF16)
+            target = ret_out if s else ret_in
+            target[s, :, :block] = (adapter_scale * jnp.dot(
+                back, down_ref[adapter_of[s]], preferred_element_type=F32)).astype(BF16)
+            target[s, :, block:] = (adapter_scale * jnp.dot(
+                mid, up_ref[adapter_of[s]], preferred_element_type=F32)).astype(BF16)
+            if s and s < half:
+                ret_near(s).start()
+            if s >= half and s % 2 == 1:
+                ret_other((s - half) // 2).start()
+            if s >= half and s % 2 == 0:
+                @pl.when(inner == 0)
+                def _():
+                    ret_same((s - half) // 2).start()
+            for a in range(resident):
+                back_m[a, lines(s), :] = (back.astype(F32) * weights[a][s]).astype(BF16)
+                inner_m[a, lines(s), :] = (mid.astype(F32) * weights[a][s]).astype(BF16)
+
+    middle = max(1, tensor_count // 2)
+    lax.fori_loop(0, middle, frozen_block, 0)
+    relay(0, 0)
+    lax.fori_loop(middle, tensor_count, frozen_block, 0)
+    for q in range(1, tensor_count):
+        part_copy(q).start()
+    relay(0, 1)
+    acc[...] = nt_dot(cot_ref[...], w_v[0])
+    for q in range(1, tensor_count):
+        cot_copy(q).wait_recv()
+    lax.fori_loop(1, middle, base_block, 0)
+    down_copy.wait()
+    up_copy.wait()
+    rank_stage(0)
+    relay(0, 2)
+    use_stage(0)
+    lax.fori_loop(middle, tensor_count, base_block, 0)
+    relay(1, 0)
+    rank_stage(1)
+    relay(1, 1)
+    use_stage(1)
+    relay(1, 2)
+    hand_back(0)
+    rank_stage(2)
+    use_stage(2)
+
+    x_all = slot_in[:, :block]
+    c_all = slot_in[:, block:]
+    for a in range(resident):
+        gd_ref[a] = tn_dot(back_m[a], x_all) * (
+            adapter_scale / jnp.maximum(jnp.full((1, block), counts[a], F32), 1.0))
+        gu_ref[a] = tn_dot(inner_m[a], c_all) * (
+            adapter_scale / jnp.maximum(jnp.full((1, out_block), counts[a], F32), 1.0))
+    gd_copy.start()
+    gu_copy.start()
+    hand_back(1)
+    for q in range(1, tensor_count):
+        part_copy(q).wait_recv()
+    backbone = parts[0].astype(F32)
+    for q in range(1, tensor_count):
+        backbone = backbone + part_in[q].astype(F32)
+    for i in range(1, dp_count - 1):
+        ret_came(i).wait_recv()
+    for j in range(seqs):
+        came = ret_in[table_ref[8 + j]]
+        kvo_ref[lines(j), :] = (backbone[lines(j)] + came[:, block:].astype(F32)).astype(BF16)
+        tg_ref[lines(j), :] = (acc[lines(j), :] + came[:, :block].astype(F32)).astype(BF16)
+
+    for k in range(1, half):
+        near_copy(k).wait_send()
+        ret_near(k).wait_send()
+    for i in range(half - 1):
+        cross_copy(i).wait_send()
+    for q in range(2):
+        ret_other(q).wait_send()
+
+        @pl.when(inner == 0)
+        def _():
+            ret_same(q).wait_send()
+
+        @pl.when(inner == 1)
+        def _():
+            for i in range(half - 1):
+                fwd_copy(q, i).wait_send()
+                back_copy(q, i).wait_send()
+    for q in range(1, tensor_count):
+        cot_copy(q).wait_send()
+        part_copy(q).wait_send()
+    gd_copy.wait()
+    gu_copy.wait()
+
+
 def finish(pieces, *refs):
     n = len(pieces)
     given, out, held = refs[:n], refs[n:2 * n], refs[2 * n:3 * n]
@@ -322,7 +752,16 @@
         move(i, p, held[i], out[i], out_sem, at).wait()
 
 
-def on_device(dp_count, tensor_count, tok, w, down, up, cot, seq_index, storage):
+def shapes_of(rows, block, out_block, resident, rank):
+    return (
+        jax.ShapeDtypeStruct((rows, out_block), BF16),
+        jax.ShapeDtypeStruct((rows, block), BF16),
+        jax.ShapeDtypeStruct((resident, rank, block), F32),
+        jax.ShapeDtypeStruct((resident, rank, out_block), F32),
+    )
+
+
+def direct(dp_count, tensor_count, tok, w, down, up, cot, seq_index, storage):
     resident, rank, block = down.shape
     out_block = up.shape[2]
     rows = tok.shape[0]
@@ -343,14 +782,9 @@
         in_specs=[smem, smem],
         out_specs=(smem, smem),
     )(seq_index, storage)
-    results = pl.pallas_call(
+    return pl.pallas_call(
         functools.partial(kernel, dp_count, tensor_count),
-        out_shape=(
-            jax.ShapeDtypeStruct((rows, out_block), BF16),
-            jax.ShapeDtypeStruct((rows, block), BF16),
-            jax.ShapeDtypeStruct((resident, rank, block), F32),
-            jax.ShapeDtypeStruct((resident, rank, out_block), F32),
-        ),
+        out_shape=shapes_of(rows, block, out_block, resident, rank),
         in_specs=[smem, smem, vmem, anywhere, anywhere, anywhere, vmem, vmem],
         out_specs=(vmem, vmem, anywhere, anywhere),
         scratch_shapes=[
@@ -384,11 +818,105 @@
             dma((groups, tensor_count)),
         ],
         compiler_params=pltpu.CompilerParams(
+            collective_id=1, has_side_effects=True, vmem_limit_bytes=60 * 1024 * 1024
+        ),
+    )(
+        table, weights, tok.reshape(seqs, length, block), w, down, up, cot,
+        cot.reshape(seqs, length, out_block))
+
+
+def relayed(dp_count, tensor_count, table, weights, tok, w, down, up, cot, seqs):
+    resident, rank, block = down.shape
+    out_block = up.shape[2]
+    rows = tok.shape[0]
+    length = rows // seqs
+    half = dp_count // 2
+    anywhere = pl.BlockSpec(memory_space=pl.ANY)
+    wide = block + out_block
+    vmem = pl.BlockSpec(memory_space=pltpu.VMEM)
+    smem = pl.BlockSpec(memory_space=pltpu.SMEM)
+    dma = pltpu.SemaphoreType.DMA
+
+    def slots(*lead):
+        return pltpu.VMEM(lead + (length, wide), BF16)
+
+    return pl.pallas_call(
+        functools.partial(relay_kernel, dp_count, tensor_count),
+        out_shape=shapes_of(rows, block, out_block, resident, rank),
+        in_specs=[smem, smem, vmem, anywhere, anywhere, anywhere, vmem, vmem],
+        out_specs=(vmem, vmem, anywhere, anywhere),
+        scratch_shapes=[
+            pltpu.VMEM(down.shape, BF16),
+            pltpu.VMEM(up.shape, BF16),
+            pltpu.VMEM(down.shape, F32),
+            pltpu.VMEM(up.shape, F32),
+            pltpu.VMEM((tensor_count, w.shape[0], out_block), BF16),
+            slots(half - 1),
+            slots(half - 1),
+            pltpu.VMEM((dp_count * length, wide), BF16),
+            slots(2, half - 1),
+            slots(2, half - 2),
+            slots(dp_count),
+            slots(dp_count - 1),
+            slots(2, half - 1),
+            slots(2, half - 1),
+            pltpu.VMEM((tensor_count, rows, out_block), BF16),
+            pltpu.VMEM((tensor_count, rows, out_block), BF16),
+            pltpu.VMEM((tensor_count, rows, out_block), BF16),
+            pltpu.VMEM((tensor_count, dp_count * length, 2 * rank), BF16),
+            pltpu.VMEM((resident, dp_count * length, rank), BF16),
+            pltpu.VMEM((resident, dp_count * length, rank), BF16),
+            pltpu.VMEM((rows, block), F32),
+            dma((tensor_count,)),
+            dma((4,)),
+            dma((half,)),
+            dma((dp_count,)),
+            dma((half - 1,)),
+            dma((2, half - 1)),
+            dma((2, half - 1)),
+            dma((dp_count,)),
+            dma((dp_count - 1,)),
+            dma((2, half - 1)),
+            dma((2, half - 1)),
+            dma((tensor_count,)),
+            dma((tensor_count,)),
+            dma((tensor_count,)),
+            dma((tensor_count,)),
+            dma((3, tensor_count)),
+            dma((3, tensor_count)),
+        ],
+        compiler_params=pltpu.CompilerParams(
             collective_id=0, has_side_effects=True, vmem_limit_bytes=60 * 1024 * 1024
         ),
     )(
         table, weights, tok.reshape(seqs, length, block), w, down, up, cot,
         cot.reshape(seqs, length, out_block))
+
+
+def on_device(dp_count, tensor_count, tok, w, down, up, cot, seq_index, storage):
+    resident = down.shape[0]
+    seqs = seq_index.shape[0] // dp_count
+    anywhere = pl.BlockSpec(memory_space=pl.ANY)
+    smem = pl.BlockSpec(memory_space=pltpu.SMEM)
+    dma = pltpu.SemaphoreType.DMA
+    args = (tok, w, down, up, cot)
+    if relay_fits(dp_count, seqs):
+        table, weights = pl.pallas_call(
+            functools.partial(relay_routes, dp_count, seqs, resident),
+            out_shape=(
+                jax.ShapeDtypeStruct((32,), jnp.int32),
+                jax.ShapeDtypeStruct((resident * dp_count + resident,), F32),
+            ),
+            in_specs=[smem, smem],
+            out_specs=(smem, smem),
+        )(seq_index, storage)
+        results = lax.cond(
+            table[7] > 0,
+            lambda: relayed(dp_count, tensor_count, table, weights, *args, seqs),
+            lambda: direct(dp_count, tensor_count, *args, seq_index, storage),
+        )
+    else:
+        results = direct(dp_count, tensor_count, *args, seq_index, storage)
     pieces = (1, 2, resident, 1)
     return pl.pallas_call(
         functools.partial(finish, pieces),

time: 71.2 us -> 79.3 us (1.11)
  Pallas kernels: 70.3 us -> 77.3 us
    pallas_call x2, Pallas kernels: 67.7 us -> 75.2 us  [the longest x1 73.6 us: relayed(): pl.pallas_call(functools.partial(relay_kernel, dp_count, tensor_count), o...]
where the time goes in v1:
time: 79.3 us; the launch traced here: 79.2 us
  Pallas kernels  77.3 us (97%)
  between operations  1.3 us (2%)
    pallas_call x1, Pallas kernels, relayed(): pl.pallas_call(functools.partial(relay_kernel, dp_count, tensor_count), o...  73.6 us
    pallas_call x1, Pallas kernels, on_device(): pl.pallas_call(functools.partial(finish, pieces), out_shape=tuple((jax.Sh...  2.1 us

profile of v1, /device:TPU:0, one launch (start us, length us, event | category | flops | bytes accessed | tf_op | source)
XLA Modules:
  0.0 79.2 jit_solution(13814073092589744729)
XLA Ops:
  0.6 1.6 %shard_map.102 = (s32[32]{0:T(128)S(1)}, f32[27]{0:T(128)S(1)}) custom-call(s32[32]{0:T(128)} %seq_ref.1, s32[24]{0:T(128)} %store_ref.1), custom_call_target="tpu_custom_call" | custom-call | tf_op jit(solution)/shard_map/pallas_call | solution.py:904
  2.2 0.6 slice.3
  3.4 73.6 %conditional.1 = ((bf16[128,512]{1,0:T(8,128)(2,1)S(1)}, bf16[128,2048]{1,0:T(8,128)(2,1)S(1)}, f32[3,64,2048]{2,1,0:T(8,128)S(1)}, f32[3,64,512]{2,1,0:T(8,128)S(1)})) conditional(s32[]{:T(128)} %bitcast.4, (s32[32]{0:T(128)}, s32[24]{0:T(128)}, bf16[128,2048]{1,0:T(8,128)(2,1)}, bf16[128,512]{1,0:T(8,128)(2,1)}, bf16[2048,2048]{1,0:T(8,128)(2,1)}, ...), branch_computations={%region_0.0_spmd, %region_1.0_spmd} | conditional | bytes 8 | solution.py:913
  3.4 73.6 %branch_1_fun.1 = (bf16[128,512]{1,0:T(8,128)(2,1)S(1)}, bf16[128,2048]{1,0:T(8,128)(2,1)S(1)}, f32[3,64,2048]{2,1,0:T(8,128)S(1)}, f32[3,64,512]{2,1,0:T(8,128)S(1)}) custom-call(s32[32]{0:T(128)S(1)} %get-tuple-element.37.table_ref, f32[27]{0:T(128)S(1)} %get-tuple-element.38.weight_ref, bf16[4,32,2048]{2,1,0:T(8,128)(2,1)} %bitcast.8, ...), custom_call_target="tpu_custom_call" | custom-call | tf_op jit(solution)/shard_map/cond/branch_1_fun/pallas_call | solution.py:843
  77.1 2.1 %shard_map.103 = (bf16[128,512]{1,0:T(8,128)(2,1)}, bf16[128,2048]{1,0:T(8,128)(2,1)}, f32[3,64,2048]{2,1,0:T(8,128)}, f32[3,64,512]{2,1,0:T(8,128)}) custom-call(bf16[128,512]{1,0:T(8,128)(2,1)S(1)} %get-tuple-element.56.refs_0_, bf16[128,2048]{1,0:T(8,128)(2,1)S(1)} %get-tuple-element.57.refs_1_, f32[3,64,2048]{2,1,0:T(8,128)S(1)} %get-tuple-element.58.refs_2_, ...), custom_call_target="tpu_custom_call" | custom-call | tf_op jit(solution)/shard_map/pallas_call | solution.py:921

commit v2 on v1

--- a/solution.py
+++ b/solution.py
@@ -318,6 +318,7 @@
     inner = lax.rem(lax.div(level + 1, jnp.int32(2)), jnp.int32(2))
     home = (2 - lax.div(d, jnp.int32(half))) * 2 + lax.rem(d, jnp.int32(2))
     zero, one = jnp.int32(0), jnp.int32(1)
+    hub = xor(d, 2 - 2 * inner)
     worst = zero
     counts = [jnp.float32(0.0)] * resident
     for k in range(dp_count):
@@ -338,7 +339,7 @@
                 for m in range(half):
                     near[m] = jnp.where(away == m, jnp.int32(j), near[m])
             if k in (0, half, half + 2):
-                step = xor(owner, home if k == 0 else d)
+                step = xor(owner, home if k == 0 else hub)
                 for m in range(half):
                     hit = step == half - 1 - m
                     has[m] = jnp.where(hit, one, has[m])
@@ -358,7 +359,7 @@
                     came = jnp.where(step == half - 1 - m, half + place[m], came)
                 table_ref[8 + j] = came
         if k in (half, half + 2):
-            q = 1 if k == half else 0
+            q = inner if k == half else 1 - inner
             table_ref[20 + 3 * q] = has[0]
             table_ref[21 + 3 * q] = has[0] * has[1]
             table_ref[22 + 3 * q] = has[3]
@@ -412,6 +413,7 @@
     w_sem,
     local_sem,
     near_ssem,
+    near_rsem,
     slot_rsem,
     cross_ssem,
     relay_rsem,
@@ -433,6 +435,7 @@
     out_block = up_ref.shape[2]
     seqs, length = tok_ref.shape[:2]
     rows = seqs * length
+    bit = length // 2
     half = dp_count // 2
     level = lax.div(d, jnp.int32(2))
     inner = lax.rem(lax.div(level + 1, jnp.int32(2)), jnp.int32(2))
@@ -441,6 +444,7 @@
     peer = [partner(d, k, dp_count) for k in range(dp_count)]
     groups = [[0, 1, 2, 3], [4, 5], [6, 7]]
     starts = [0, 4, 6]
+    close, far = 0, 1
 
     def t_to(q):
         return lax.rem(t + q, tensor_count)
@@ -463,48 +467,62 @@
         return pltpu.make_async_remote_copy(
             source, target, ssem, rsem, device_id=where, device_id_type=MESH)
 
-    def slot_at(s):
-        return slot_in.at[pl.ds(s * length, length)]
+    def piece(h):
+        return pl.ds(h * bit, bit)
+
+    def slot_at(s, h):
+        return slot_in.at[pl.ds(s * length + h * bit, bit)]
 
     def near_copy(k):
-        return over(near_out.at[k - 1], slot_at(k), near_ssem.at[k], slot_rsem.at[k], dp=peer[k])
-
-    def cross_copy(i):
-        return over(cross_out.at[i], relay_in.at[outer, i], cross_ssem.at[i], relay_rsem.at[outer, i], dp=home)
-
-    def cross_came(q, i):
-        return over(cross_out.at[i], relay_in.at[q, i], cross_ssem.at[i], relay_rsem.at[q, i], dp=home)
-
-    def fwd_copy(q, m):
-        source = relay_in.at[q, 0] if m == 0 else relay_out.at[q, m - 1]
+        return over(near_out.at[k - 1], slot_in.at[pl.ds(k * length, length)],
+                    near_ssem.at[k], near_rsem.at[k], dp=peer[k])
+
+    def cross_copy(i, h):
+        return over(cross_out.at[i, piece(h)], relay_in.at[outer, i, piece(h)],
+                    cross_ssem.at[i, h], relay_rsem.at[outer, i, h], dp=home)
+
+    def cross_came(q, i, h):
+        return over(cross_out.at[i, piece(h)], relay_in.at[q, i, piece(h)],
+                    cross_ssem.at[i, h], relay_rsem.at[q, i, h], dp=home)
+
+    def fwd_copy(q, m, h):
+        source = relay_in.at[q, 0, piece(h)] if m == 0 else relay_out.at[q, m - 1, piece(h)]
         s = half + 2 * q + (0 if m == 1 else 1)
-        return over(source, slot_at(s), fwd_ssem.at[q, m], slot_rsem.at[s], dp=peer[3 - m])
-
-    def slot_came(s):
-        return over(near_out.at[0], slot_at(s), near_ssem.at[0], slot_rsem.at[s], dp=peer[1])
+        return over(source, slot_at(s, h), fwd_ssem.at[q, m, h], slot_rsem.at[s - half, h], dp=peer[3 - m])
+
+    def slot_came(s, h):
+        return over(near_out.at[0, piece(h)], slot_at(s, h), near_ssem.at[0], slot_rsem.at[s - half, h], dp=peer[1])
 
     def ret_near(k):
-        return over(ret_out.at[k], ret_in.at[k], ret_ssem.at[k], ret_rsem.at[k], dp=peer[k])
-
-    def ret_same(q):
+        return over(ret_out.at[k], ret_in.at[k], ret_ssem.at[k, 0], ret_rsem.at[k, 0], dp=peer[k])
+
+    def ret_same(q, h):
         s = half + 2 * q
-        return over(ret_out.at[s], relay_ret.at[q, 1], ret_ssem.at[s], owner_rsem.at[q, 1], dp=peer[2])
-
-    def ret_other(q):
+        return over(ret_out.at[s, piece(h)], relay_ret.at[q, 1, piece(h)],
+                    ret_ssem.at[s, h], owner_rsem.at[q, 1, h], dp=peer[2])
+
+    def ret_other(q, h):
         s = half + 2 * q + 1
-        m = 2 * inner
-        return over(ret_out.at[s], relay_ret.at[q, m], ret_ssem.at[s], owner_rsem.at[q, m],
-                    dp=inner * peer[1] + outer * peer[3])
-
-    def owner_came(q, m):
-        return over(ret_out.at[1], relay_ret.at[q, m], ret_ssem.at[1], owner_rsem.at[q, m], dp=peer[1])
-
-    def back_copy(q, i):
-        return over(back_out.at[q, i], ret_in.at[half + i], back_ssem.at[q, i], ret_rsem.at[half + i],
+        return over(ret_out.at[s, piece(h)], relay_ret.at[q, 2, piece(h)],
+                    ret_ssem.at[s, h], owner_rsem.at[q, 2, h], dp=peer[1])
+
+    def ret_merged(q, h):
+        return over(back_out.at[q, 0, piece(h)], relay_ret.at[q, 0, piece(h)],
+                    back_ssem.at[q, 0, h], owner_rsem.at[q, 0, h], dp=peer[2])
+
+    def owner_came(q, m, h):
+        return over(ret_out.at[1, piece(h)], relay_ret.at[q, m, piece(h)],
+                    ret_ssem.at[1, h], owner_rsem.at[q, m, h], dp=peer[1])
+
+    def back_copy(q, i, h):
+        source = relay_ret.at[q, 0, piece(h)] if i == 0 else back_out.at[q, i, piece(h)]
+        return over(source, ret_in.at[half + i, piece(h)],
+                    back_ssem.at[q, i, h], ret_rsem.at[half + i, h],
                     dp=peer[half + 2 - 2 * q])
 
-    def ret_came(i):
-        return over(ret_out.at[1], ret_in.at[i], ret_ssem.at[1], ret_rsem.at[i], dp=peer[1])
+    def back_came(i, h):
+        return over(ret_out.at[1, piece(h)], ret_in.at[half + i, piece(h)],
+                    ret_ssem.at[1, h], ret_rsem.at[half + i, h], dp=peer[1])
 
     def cot_copy(q):
         return over(cot_ref, cots.at[q], cot_ssem.at[q], cot_rsem.at[q], tensor=t_to(q))
@@ -529,8 +547,13 @@
     gu_copy = pltpu.make_async_copy(gu_ref, gu_hbm, local_sem.at[3])
 
     barrier = pltpu.get_barrier_semaphore()
-    for k in range(1, dp_count):
+    for k in range(1, half + 1):
         pl.semaphore_signal(barrier, inc=1, device_id={"dp": peer[k]}, device_id_type=MESH)
+
+    @pl.when(inner == 1)
+    def _():
+        pl.semaphore_signal(barrier, inc=1, device_id={"dp": peer[half + 2]}, device_id_type=MESH)
+
     for q in range(1, tensor_count):
         pl.semaphore_signal(barrier, inc=1, device_id={"tensor": t_to(q)}, device_id_type=MESH)
     for i in range(tensor_count):
@@ -551,22 +574,13 @@
             near_out[k - 1, :, :block] = tok_ref[pick]
             near_out[k - 1, :, block:] = cot_seq_ref[pick]
 
-    pl.semaphore_wait(barrier, dp_count + tensor_count - 2)
-
-    @pl.when(inner == 1)
-    def _():
-        for i in range(half - 1):
-            cross_copy(i).start()
-        for k in (3, 2, 1):
-            near_copy(k).start()
-
-    @pl.when(inner == 0)
-    def _():
-        for k in (3, 2, 1):
-            near_copy(k).start()
-        for i in range(half - 1):
-            cross_copy(i).start()
-
+    pl.semaphore_wait(barrier, half + inner + tensor_count - 1)
+
+    for i in range(half - 1):
+        for h in range(2):
+            cross_copy(i, h).start()
+    for k in (3, 2, 1):
+        near_copy(k).start()
     for q in range(1, tensor_count):
         cot_copy(q).start()
 
@@ -578,29 +592,40 @@
     def relay(q, i):
         @pl.when(inner == 1)
         def _():
-            cross_came(q, i).wait_recv()
-            if i == 0:
-                fwd_copy(q, 0).start()
-            if i == 1:
-                relay_out[q, 0] = mix(relay_in[q, 1], relay_in[q, 0], flags[q][0])
-                fwd_copy(q, 1).start()
+            for h in range(2):
+                at = slice(h * bit, (h + 1) * bit)
+                cross_came(q, i, h).wait_recv()
+                if i == 1:
+                    relay_out[q, 0, at] = mix(relay_in[q, 1, at], relay_in[q, 0, at], flags[q][0])
+                if i == 2:
+                    relay_out[q, 1, at] = mix(relay_in[q, 1, at], relay_in[q, 2, at], flags[q][2])
+                fwd_copy(q, i, h).start()
             if i == 2:
-                relay_out[q, 1] = mix(relay_in[q, 1], relay_in[q, 2], flags[q][2])
-                fwd_copy(q, 2).start()
                 slot_in[lines(half + 2 * q), :] = relay_in[q, 2]
 
-    def hand_back(q):
+    def hand_back(q, i):
         @pl.when(inner == 1)
         def _():
-            owner_came(q, 0).wait_recv()
-            owner_came(q, 1).wait_recv()
-            back_out[q, 0] = mix(relay_ret[q, 0], relay_ret[q, 1], flags[q][0])
-            back_copy(q, 0).start()
-            owner_came(q, 2).wait_recv()
-            back_out[q, 1] = mix(relay_ret[q, 1], relay_ret[q, 2], flags[q][1])
-            back_copy(q, 1).start()
-            back_out[q, 2] = mix(ret_out[half + 2 * q], relay_ret[q, 2], flags[q][2])
-            back_copy(q, 2).start()
+            for h in range(2):
+                at = slice(h * bit, (h + 1) * bit)
+                if i == 0:
+                    owner_came(q, 0, h).wait_recv()
+                if i == 1:
+                    owner_came(q, 1, h).wait_recv()
+                    owner_came(q, 2, h).wait_recv()
+                    back_out[q, 1, at] = mix(relay_ret[q, 1, at], relay_ret[q, 2, at], flags[q][1])
+                if i == 2:
+                    back_out[q, 2, at] = mix(ret_out[half + 2 * q, at], relay_ret[q, 2, at], flags[q][2])
+                back_copy(q, i, h).start()
+
+    def merge_out(q):
+        @pl.when(inner == 0)
+        def _():
+            for h in range(2):
+                at = slice(h * bit, (h + 1) * bit)
+                owner_came(q, 2, h).wait_recv()
+                back_out[q, 0, at] = mix(relay_ret[q, 2, at], ret_out[half + 2 * q, at], flags[q][0])
+                ret_merged(q, h).start()
 
     def frozen_block(i, carry):
         w_copy(i).wait()
@@ -615,13 +640,15 @@
     def rank_stage(g):
         for s in groups[g]:
             if s and s < half:
-                slot_came(s).wait_recv()
+                near_copy(s).wait_recv()
             if s >= half and s % 2 == 1:
-                slot_came(s).wait_recv()
+                for h in range(2):
+                    slot_came(s, h).wait_recv()
             if s >= half and s % 2 == 0:
                 @pl.when(inner == 0)
                 def _():
-                    slot_came(s).wait_recv()
+                    for h in range(2):
+                        slot_came(s, h).wait_recv()
         for s in groups[g]:
             x = slot_in[lines(s), :block]
             c = slot_in[lines(s), block:]
@@ -648,43 +675,50 @@
                 back, down_ref[adapter_of[s]], preferred_element_type=F32)).astype(BF16)
             target[s, :, block:] = (adapter_scale * jnp.dot(
                 mid, up_ref[adapter_of[s]], preferred_element_type=F32)).astype(BF16)
-            if s and s < half:
-                ret_near(s).start()
-            if s >= half and s % 2 == 1:
-                ret_other((s - half) // 2).start()
-            if s >= half and s % 2 == 0:
-                @pl.when(inner == 0)
-                def _():
-                    ret_same((s - half) // 2).start()
             for a in range(resident):
                 back_m[a, lines(s), :] = (back.astype(F32) * weights[a][s]).astype(BF16)
                 inner_m[a, lines(s), :] = (mid.astype(F32) * weights[a][s]).astype(BF16)
+        if g:
+            q = g - 1
+            for h in range(2):
+                ret_other(q, h).start()
+
+            @pl.when(inner == 0)
+            def _():
+                for h in range(2):
+                    ret_same(q, h).start()
 
     middle = max(1, tensor_count // 2)
     lax.fori_loop(0, middle, frozen_block, 0)
-    relay(0, 0)
     lax.fori_loop(middle, tensor_count, frozen_block, 0)
     for q in range(1, tensor_count):
         part_copy(q).start()
-    relay(0, 1)
     acc[...] = nt_dot(cot_ref[...], w_v[0])
+    relay(far, 0)
     for q in range(1, tensor_count):
         cot_copy(q).wait_recv()
     lax.fori_loop(1, middle, base_block, 0)
     down_copy.wait()
     up_copy.wait()
+    relay(far, 1)
+    lax.fori_loop(middle, tensor_count, base_block, 0)
+    relay(far, 2)
+    relay(close, 0)
+    rank_stage(2)
+    relay(close, 1)
     rank_stage(0)
-    relay(0, 2)
+    use_stage(2)
+    relay(close, 2)
     use_stage(0)
-    lax.fori_loop(middle, tensor_count, base_block, 0)
-    relay(1, 0)
+    merge_out(far)
+    hand_back(far, 0)
+    hand_back(far, 1)
+    hand_back(far, 2)
     rank_stage(1)
-    relay(1, 1)
     use_stage(1)
-    relay(1, 2)
-    hand_back(0)
-    rank_stage(2)
-    use_stage(2)
+    merge_out(close)
+    for k in (3, 2, 1):
+        ret_near(k).start()
 
     x_all = slot_in[:, :block]
     c_all = slot_in[:, block:]
@@ -695,14 +729,18 @@
             adapter_scale / jnp.maximum(jnp.full((1, out_block), counts[a], F32), 1.0))
     gd_copy.start()
     gu_copy.start()
-    hand_back(1)
+    for i in range(half - 1):
+        hand_back(close, i)
     for q in range(1, tensor_count):
         part_copy(q).wait_recv()
     backbone = parts[0].astype(F32)
     for q in range(1, tensor_count):
         backbone = backbone + part_in[q].astype(F32)
-    for i in range(1, dp_count - 1):
-        ret_came(i).wait_recv()
+    for k in range(1, half):
+        ret_near(k).wait_recv()
+    for i in range(half - 1):
+        for h in range(2):
+            back_came(i, h).wait_recv()
     for j in range(seqs):
         came = ret_in[table_ref[8 + j]]
         kvo_ref[lines(j), :] = (backbone[lines(j)] + came[:, block:].astype(F32)).astype(BF16)
@@ -711,20 +749,27 @@
     for k in range(1, half):
         near_copy(k).wait_send()
         ret_near(k).wait_send()
-    for i in range(half - 1):
-        cross_copy(i).wait_send()
-    for q in range(2):
-        ret_other(q).wait_send()
-
-        @pl.when(inner == 0)
-        def _():
-            ret_same(q).wait_send()
-
-        @pl.when(inner == 1)
-        def _():
+    for h in range(2):
+        for i in range(half - 1):
+            cross_copy(i, h).wait_send()
+        for q in range(2):
+            ret_other(q, h).wait_send()
+
+    @pl.when(inner == 0)
+    def _():
+        for q in range(2):
+            for h in range(2):
+                ret_same(q, h).wait_send()
+                ret_merged(q, h).wait_send()
+
+    @pl.when(inner == 1)
+    def _():
+        for q in range(2):
             for i in range(half - 1):
-                fwd_copy(q, i).wait_send()
-                back_copy(q, i).wait_send()
+                for h in range(2):
+                    fwd_copy(q, i, h).wait_send()
+                    back_copy(q, i, h).wait_send()
+
     for q in range(1, tensor_count):
         cot_copy(q).wait_send()
         part_copy(q).wait_send()
@@ -734,22 +779,18 @@
 
 def finish(pieces, *refs):
     n = len(pieces)
-    given, out, held = refs[:n], refs[n:2 * n], refs[2 * n:3 * n]
-    in_sem, out_sem = refs[3 * n:]
+    given, out, sem = refs[:n], refs[n:2 * n], refs[2 * n]
     steps = [(i, p) for i in range(n) for p in range(pieces[i])]
 
-    def move(i, p, source, target, sem, at):
-        span = source.shape[0] // pieces[i]
+    def move(at, i, p):
+        span = given[i].shape[0] // pieces[i]
         rows = pl.ds(p * span, span)
-        return pltpu.make_async_copy(source.at[rows], target.at[rows], sem.at[at])
+        return pltpu.make_async_copy(given[i].at[rows], out[i].at[rows], sem.at[at])
 
     for at, (i, p) in enumerate(steps):
-        move(i, p, given[i], held[i], in_sem, at).start()
+        move(at, i, p).start()
     for at, (i, p) in enumerate(steps):
-        move(i, p, given[i], held[i], in_sem, at).wait()
-        move(i, p, held[i], out[i], out_sem, at).start()
-    for at, (i, p) in enumerate(steps):
-        move(i, p, held[i], out[i], out_sem, at).wait()
+        move(at, i, p).wait()
 
 
 def shapes_of(rows, block, out_block, resident, rank):
@@ -870,14 +911,15 @@
             dma((tensor_count,)),
             dma((4,)),
             dma((half,)),
-            dma((dp_count,)),
-            dma((half - 1,)),
-            dma((2, half - 1)),
-            dma((2, half - 1)),
-            dma((dp_count,)),
-            dma((dp_count - 1,)),
-            dma((2, half - 1)),
-            dma((2, half - 1)),
+            dma((half,)),
+            dma((half, 2)),
+            dma((half - 1, 2)),
+            dma((2, half - 1, 2)),
+            dma((2, half - 1, 2)),
+            dma((dp_count, 2)),
+            dma((dp_count - 1, 2)),
+            dma((2, half - 1, 2)),
+            dma((2, half - 1, 2)),
             dma((tensor_count,)),
             dma((tensor_count,)),
             dma((tensor_count,)),
@@ -897,6 +939,7 @@
     resident = down.shape[0]
     seqs = seq_index.shape[0] // dp_count
     anywhere = pl.BlockSpec(memory_space=pl.ANY)
+    vmem = pl.BlockSpec(memory_space=pltpu.VMEM)
     smem = pl.BlockSpec(memory_space=pltpu.SMEM)
     dma = pltpu.SemaphoreType.DMA
     args = (tok, w, down, up, cot)
@@ -921,10 +964,9 @@
     return pl.pallas_call(
         functools.partial(finish, pieces),
         out_shape=tuple(jax.ShapeDtypeStruct(r.shape, r.dtype) for r in results),
-        in_specs=[anywhere] * 4,
+        in_specs=[vmem] * 4,
         out_specs=(anywhere,) * 4,
-        scratch_shapes=[pltpu.VMEM(r.shape, r.dtype) for r in results] + [
-            dma((sum(pieces),)), dma((sum(pieces),))],
+        scratch_shapes=[dma((sum(pieces),))],
     )(*results)
 
 

time: 79.3 us -> 62.7 us (0.79)
  the two profiles are of different devices: /device:TPU:0 before, /device:TPU:8 now
where the time goes in v2:
time: 62.7 us; the launch traced here: 62.6 us
  Pallas kernels  60.7 us (97%)
  between operations  1.3 us (2%)
    pallas_call x1, Pallas kernels, relayed(): pl.pallas_call(functools.partial(relay_kernel, dp_count, tensor_count), o...  57.6 us
    pallas_call x1, Pallas kernels, on_device(): pl.pallas_call(functools.partial(relay_routes, dp_count, seqs, resident),...  1.56 us
    pallas_call x1, Pallas kernels, on_device(): pl.pallas_call(functools.partial(finish, pieces), out_shape=tuple((jax.Sh...  1.54 us

profile of v2, /device:TPU:8, one launch (start us, length us, event | category | flops | bytes accessed | tf_op | source)
XLA Modules:
  0.0 62.6 jit_solution(139101331622161131)
XLA Ops:
  0.6 1.6 %shard_map.102 = (s32[32]{0:T(128)S(1)}, f32[27]{0:T(128)S(1)}) custom-call(s32[32]{0:T(128)} %seq_ref.1, s32[24]{0:T(128)} %store_ref.1), custom_call_target="tpu_custom_call" | custom-call | tf_op jit(solution)/shard_map/pallas_call | solution.py:947
  2.2 0.6 slice.3
  3.4 57.6 %conditional.1 = ((bf16[128,512]{1,0:T(8,128)(2,1)S(1)}, bf16[128,2048]{1,0:T(8,128)(2,1)S(1)}, f32[3,64,2048]{2,1,0:T(8,128)S(1)}, f32[3,64,512]{2,1,0:T(8,128)S(1)})) conditional(s32[]{:T(128)} %bitcast.4, (s32[32]{0:T(128)}, s32[24]{0:T(128)}, bf16[128,2048]{1,0:T(8,128)(2,1)}, bf16[128,512]{1,0:T(8,128)(2,1)}, bf16[2048,2048]{1,0:T(8,128)(2,1)}, ...), branch_computations={%region_0.0_spmd, %region_1.0_spmd} | conditional | bytes 8 | solution.py:956
  3.5 57.6 %branch_1_fun.1 = (bf16[128,512]{1,0:T(8,128)(2,1)S(1)}, bf16[128,2048]{1,0:T(8,128)(2,1)S(1)}, f32[3,64,2048]{2,1,0:T(8,128)S(1)}, f32[3,64,512]{2,1,0:T(8,128)S(1)}) custom-call(s32[32]{0:T(128)S(1)} %get-tuple-element.37.table_ref, f32[27]{0:T(128)S(1)} %get-tuple-element.38.weight_ref, bf16[4,32,2048]{2,1,0:T(8,128)(2,1)} %bitcast.8, ...), custom_call_target="tpu_custom_call" | custom-call | tf_op jit(solution)/shard_map/cond/branch_1_fun/pallas_call | solution.py:884
  61.0 1.5 %shard_map.103 = (bf16[128,512]{1,0:T(8,128)(2,1)}, bf16[128,2048]{1,0:T(8,128)(2,1)}, f32[3,64,2048]{2,1,0:T(8,128)}, f32[3,64,512]{2,1,0:T(8,128)}) custom-call(bf16[128,512]{1,0:T(8,128)(2,1)S(1)} %get-tuple-element.56.refs_0_, bf16[128,2048]{1,0:T(8,128)(2,1)S(1)} %get-tuple-element.57.refs_1_, f32[3,64,2048]{2,1,0:T(8,128)S(1)} %get-tuple-element.58.refs_2_, ...), custom_call_target="tpu_custom_call" | custom-call | tf_op jit(solution)/shard_map/pallas_call | solution.py:964

commit v3 on v2

--- a/solution.py
+++ b/solution.py
@@ -310,7 +310,7 @@
     return dp_count == 2 * seqs and seqs == 4
 
 
-def relay_routes(dp_count, seqs, resident, seq_ref, store_ref, table_ref, weight_ref):
+def relay_routes(dp_count, seqs, resident, seq_ref, store_ref, table_ref, weight_ref, fits_ref):
     d = lax.axis_index("dp")
     half = dp_count // 2
     xor = lax.bitwise_xor
@@ -371,7 +371,7 @@
             counts[a] = counts[a] + hit
     for a in range(resident):
         weight_ref[resident * dp_count + a] = counts[a]
-    table_ref[7] = jnp.where(worst < half, one, zero)
+    fits_ref[0] = jnp.where(worst < half, one, zero)
 
 
 def relay_kernel(
@@ -379,12 +379,11 @@
     tensor_count,
     table_ref,
     weight_ref,
-    tok_ref,
+    tok_hbm,
     w_ref,
     down_hbm,
     up_hbm,
-    cot_ref,
-    cot_seq_ref,
+    cot_hbm,
     kvo_ref,
     tg_ref,
     gd_hbm,
@@ -393,35 +392,33 @@
     up_ref,
     gd_ref,
     gu_ref,
+    tok_ref,
+    cot_ref,
     w_v,
     near_out,
     cross_out,
+    stage_in,
     slot_in,
-    relay_in,
     relay_out,
-    ret_out,
+    bulk,
     ret_in,
-    relay_ret,
-    back_out,
     cots,
     parts,
     part_in,
     ranks,
+    ranks_in,
     back_m,
     inner_m,
     acc,
     w_sem,
     local_sem,
-    near_ssem,
+    send_sem,
     near_rsem,
     slot_rsem,
-    cross_ssem,
     relay_rsem,
-    fwd_ssem,
-    ret_ssem,
+    stage_rsem,
+    owner_rsem,
     ret_rsem,
-    owner_rsem,
-    back_ssem,
     cot_ssem,
     cot_rsem,
     part_ssem,
@@ -440,11 +437,14 @@
     level = lax.div(d, jnp.int32(2))
     inner = lax.rem(lax.div(level + 1, jnp.int32(2)), jnp.int32(2))
     outer = 1 - inner
-    home = (2 - lax.div(d, jnp.int32(half))) * 2 + lax.rem(d, jnp.int32(2))
     peer = [partner(d, k, dp_count) for k in range(dp_count)]
     groups = [[0, 1, 2, 3], [4, 5], [6, 7]]
     starts = [0, 4, 6]
     close, far = 0, 1
+
+    ret_out = bulk.at[pl.ds(0, dp_count)]
+    relay_ret, back_out, relay_in = (
+        bulk.at[pl.ds(dp_count + 2 * (half - 1) * n, 2 * (half - 1))] for n in range(3))
 
     def t_to(q):
         return lax.rem(t + q, tensor_count)
@@ -474,77 +474,102 @@
         return slot_in.at[pl.ds(s * length + h * bit, bit)]
 
     def near_copy(k):
-        return over(near_out.at[k - 1], slot_in.at[pl.ds(k * length, length)],
-                    near_ssem.at[k], near_rsem.at[k], dp=peer[k])
+        return over(near_out.at[k - 1], slot_in.at[pl.ds(k * length, length)], send_sem, near_rsem, dp=peer[k])
+
+    def near_came():
+        at = slot_in.at[pl.ds(length, (half - 1) * length)]
+        return over(at, at, send_sem, near_rsem, dp=peer[1])
 
     def cross_copy(i, h):
-        return over(cross_out.at[i, piece(h)], relay_in.at[outer, i, piece(h)],
-                    cross_ssem.at[i, h], relay_rsem.at[outer, i, h], dp=home)
+        return over(cross_out.at[i, piece(h)], relay_in.at[i, piece(h)],
+                    send_sem, relay_rsem.at[close, i, h], dp=peer[half + 2])
+
+    def stage_copy(i, h):
+        return over(cross_out.at[i, piece(h)], stage_in.at[i, piece(h)], send_sem, stage_rsem.at[i, h], dp=peer[2])
+
+    def onward_copy(i, h):
+        return over(stage_in.at[i, piece(h)], relay_in.at[half - 1 + i, piece(h)],
+                    send_sem, relay_rsem.at[far, i, h], dp=peer[half + 2])
 
     def cross_came(q, i, h):
-        return over(cross_out.at[i, piece(h)], relay_in.at[q, i, piece(h)],
-                    cross_ssem.at[i, h], relay_rsem.at[q, i, h], dp=home)
+        at = relay_in.at[(half - 1) * q + i, piece(h)]
+        return over(at, at, send_sem, relay_rsem.at[q, i, h], dp=peer[half + 2])
 
     def fwd_copy(q, m, h):
-        source = relay_in.at[q, 0, piece(h)] if m == 0 else relay_out.at[q, m - 1, piece(h)]
         s = half + 2 * q + (0 if m == 1 else 1)
-        return over(source, slot_at(s, h), fwd_ssem.at[q, m, h], slot_rsem.at[s - half, h], dp=peer[3 - m])
-
-    def slot_came(s, h):
-        return over(near_out.at[0, piece(h)], slot_at(s, h), near_ssem.at[0], slot_rsem.at[s - half, h], dp=peer[1])
+        source = relay_out.at[q, m - 1, piece(h)] if m else relay_in.at[(half - 1) * q, piece(h)]
+        return over(source, slot_at(s, h), send_sem, slot_rsem.at[s - half], dp=peer[3 - m])
+
+    def slot_came(s):
+        at = slot_in.at[pl.ds(s * length, length)]
+        return over(at, at, send_sem, slot_rsem.at[s - half], dp=peer[1])
 
     def ret_near(k):
-        return over(ret_out.at[k], ret_in.at[k], ret_ssem.at[k, 0], ret_rsem.at[k, 0], dp=peer[k])
+        return over(ret_out.at[k], ret_in.at[k], send_sem, ret_rsem, dp=peer[k])
 
     def ret_same(q, h):
-        s = half + 2 * q
-        return over(ret_out.at[s, piece(h)], relay_ret.at[q, 1, piece(h)],
-                    ret_ssem.at[s, h], owner_rsem.at[q, 1, h], dp=peer[2])
+        return over(ret_out.at[half + 2 * q, piece(h)], relay_ret.at[(half - 1) * q + 1, piece(h)],
+                    send_sem, owner_rsem.at[q, 1, h], dp=peer[2])
 
     def ret_other(q, h):
-        s = half + 2 * q + 1
-        return over(ret_out.at[s, piece(h)], relay_ret.at[q, 2, piece(h)],
-                    ret_ssem.at[s, h], owner_rsem.at[q, 2, h], dp=peer[1])
+        return over(ret_out.at[half + 2 * q + 1, piece(h)], relay_ret.at[(half - 1) * q + 2, piece(h)],
+                    send_sem, owner_rsem.at[q, 2, h], dp=peer[1])
 
     def ret_merged(q, h):
-        return over(back_out.at[q, 0, piece(h)], relay_ret.at[q, 0, piece(h)],
-                    back_ssem.at[q, 0, h], owner_rsem.at[q, 0, h], dp=peer[2])
+        return over(back_out.at[(half - 1) * q, piece(h)], relay_ret.at[(half - 1) * q, piece(h)],
+                    send_sem, owner_rsem.at[q, 0, h], dp=peer[2])
 
     def owner_came(q, m, h):
-        return over(ret_out.at[1, piece(h)], relay_ret.at[q, m, piece(h)],
-                    ret_ssem.at[1, h], owner_rsem.at[q, m, h], dp=peer[1])
+        at = relay_ret.at[(half - 1) * q + m, piece(h)]
+        return over(at, at, send_sem, owner_rsem.at[q, m, h], dp=peer[1])
 
     def back_copy(q, i, h):
-        source = relay_ret.at[q, 0, piece(h)] if i == 0 else back_out.at[q, i, piece(h)]
-        return over(source, ret_in.at[half + i, piece(h)],
-                    back_ssem.at[q, i, h], ret_rsem.at[half + i, h],
-                    dp=peer[half + 2 - 2 * q])
-
-    def back_came(i, h):
-        return over(ret_out.at[1, piece(h)], ret_in.at[half + i, piece(h)],
-                    ret_ssem.at[1, h], ret_rsem.at[half + i, h], dp=peer[1])
+        source = (back_out if i else relay_ret).at[(half - 1) * q + i, piece(h)]
+        return over(source, ret_in.at[half + i, piece(h)], send_sem, ret_rsem, dp=peer[half + 2 - 2 * q])
+
+    def rets_came():
+        at = ret_in.at[pl.ds(1, 2 * half - 2)]
+        return over(at, at, send_sem, ret_rsem, dp=peer[1])
+
+    def sent(count):
+        return over(bulk.at[pl.ds(0, count)], bulk.at[pl.ds(0, count)], send_sem, ret_rsem, dp=peer[1])
 
     def cot_copy(q):
-        return over(cot_ref, cots.at[q], cot_ssem.at[q], cot_rsem.at[q], tensor=t_to(q))
+        return over(cot_ref, cots.at[q], cot_ssem, cot_rsem, tensor=t_to(q))
+
+    def cots_came():
+        at = cots.at[pl.ds(1, tensor_count - 1)]
+        return over(at, at, cot_ssem, cot_rsem, tensor=t_to(1))
 
     def part_copy(q):
-        return over(parts.at[q], part_in.at[q], part_ssem.at[q], part_rsem.at[q], tensor=t_to(q))
+        return over(parts.at[q], part_in.at[q], part_ssem, part_rsem, tensor=t_to(q))
+
+    def parts_came():
+        at = part_in.at[pl.ds(1, tensor_count - 1)]
+        return over(at, at, part_ssem, part_rsem, tensor=t_to(1))
 
     def rank_rows(g):
         return pl.ds(starts[g] * length, len(groups[g]) * length)
 
     def rank_copy(g, q):
-        at = ranks.at[t, rank_rows(g)]
-        return over(at, at, rank_ssem.at[g, q], rank_rsem.at[g, q], tensor=t_to(q))
-
-    def rank_came(g, q):
-        at = ranks.at[t_from(q), rank_rows(g)]
-        return over(at, at, rank_ssem.at[g, q], rank_rsem.at[g, q], tensor=t_to(q))
+        return over(ranks.at[rank_rows(g)], ranks_in.at[q - 1, rank_rows(g)], rank_ssem, rank_rsem.at[g], tensor=t_to(q))
+
+    def ranks_came(g):
+        at = ranks_in.at[:, rank_rows(g)]
+        return over(at, at, rank_ssem, rank_rsem.at[g], tensor=t_to(1))
+
+    def ranks_sent():
+        return over(ranks_in, ranks_in, rank_ssem, rank_rsem.at[0], tensor=t_to(1))
 
     down_copy = pltpu.make_async_copy(down_hbm, down_ref, local_sem.at[0])
     up_copy = pltpu.make_async_copy(up_hbm, up_ref, local_sem.at[1])
     gd_copy = pltpu.make_async_copy(gd_ref, gd_hbm, local_sem.at[2])
     gu_copy = pltpu.make_async_copy(gu_ref, gu_hbm, local_sem.at[3])
+
+    tok_copy = pltpu.make_async_copy(tok_hbm, tok_ref, local_sem.at[4])
+    seed_copy = pltpu.make_async_copy(cot_hbm, cot_ref, local_sem.at[5])
+    tok_copy.start()
+    seed_copy.start()
 
     barrier = pltpu.get_barrier_semaphore()
     for k in range(1, half + 1):
@@ -560,27 +585,40 @@
         w_copy(i).start()
     down_copy.start()
     up_copy.start()
+    tok_copy.wait()
+    seed_copy.wait()
 
     for i in range(half - 1):
         pick = table_ref[half + i]
         cross_out[i, :, :block] = tok_ref[pick]
-        cross_out[i, :, block:] = cot_seq_ref[pick]
+        cross_out[i, :, block:] = cot_ref[pick]
     for k in range(half):
         pick = table_ref[k]
         if k == 0:
             slot_in[:length, :block] = tok_ref[pick]
-            slot_in[:length, block:] = cot_seq_ref[pick]
+            slot_in[:length, block:] = cot_ref[pick]
         else:
             near_out[k - 1, :, :block] = tok_ref[pick]
-            near_out[k - 1, :, block:] = cot_seq_ref[pick]
+            near_out[k - 1, :, block:] = cot_ref[pick]
 
     pl.semaphore_wait(barrier, half + inner + tensor_count - 1)
 
-    for i in range(half - 1):
-        for h in range(2):
-            cross_copy(i, h).start()
-    for k in (3, 2, 1):
-        near_copy(k).start()
+    @pl.when(inner == 1)
+    def _():
+        for i in range(half - 1):
+            for h in range(2):
+                cross_copy(i, h).start()
+
+    @pl.when(inner == 0)
+    def _():
+        near_copy(3).start()
+        for i in range(half - 1):
+            for h in range(2):
+                stage_copy(i, h).start()
+
+    near_copy(1).start()
+    near_copy(2).start()
+
     for q in range(1, tensor_count):
         cot_copy(q).start()
 
@@ -589,42 +627,52 @@
     weights = [[weight_ref[a * dp_count + s] for s in range(dp_count)] for a in range(resident)]
     counts = [weight_ref[resident * dp_count + a] for a in range(resident)]
 
+    def onward(i):
+        @pl.when(inner == 1)
+        def _():
+            for h in range(2):
+                stage_copy(i, h).wait_recv()
+                onward_copy(i, h).start()
+
     def relay(q, i):
+        base = (half - 1) * q
+
         @pl.when(inner == 1)
         def _():
             for h in range(2):
                 at = slice(h * bit, (h + 1) * bit)
                 cross_came(q, i, h).wait_recv()
                 if i == 1:
-                    relay_out[q, 0, at] = mix(relay_in[q, 1, at], relay_in[q, 0, at], flags[q][0])
+                    relay_out[q, 0, at] = mix(relay_in[base + 1, at], relay_in[base, at], flags[q][0])
                 if i == 2:
-                    relay_out[q, 1, at] = mix(relay_in[q, 1, at], relay_in[q, 2, at], flags[q][2])
+                    relay_out[q, 1, at] = mix(relay_in[base + 1, at], relay_in[base + 2, at], flags[q][2])
                 fwd_copy(q, i, h).start()
             if i == 2:
-                slot_in[lines(half + 2 * q), :] = relay_in[q, 2]
+                slot_in[lines(half + 2 * q), :] = relay_in[base + 2]
 
     def hand_back(q, i):
+        base = (half - 1) * q
+
         @pl.when(inner == 1)
         def _():
             for h in range(2):
                 at = slice(h * bit, (h + 1) * bit)
-                if i == 0:
-                    owner_came(q, 0, h).wait_recv()
+                owner_came(q, i, h).wait_recv()
                 if i == 1:
-                    owner_came(q, 1, h).wait_recv()
-                    owner_came(q, 2, h).wait_recv()
-                    back_out[q, 1, at] = mix(relay_ret[q, 1, at], relay_ret[q, 2, at], flags[q][1])
+                    back_out[base + 1, at] = mix(relay_ret[base + 1, at], relay_ret[base + 2, at], flags[q][1])
                 if i == 2:
-                    back_out[q, 2, at] = mix(ret_out[half + 2 * q, at], relay_ret[q, 2, at], flags[q][2])
+                    back_out[base + 2, at] = mix(ret_out[half + 2 * q, at], relay_ret[base + 2, at], flags[q][2])
                 back_copy(q, i, h).start()
 
     def merge_out(q):
+        base = (half - 1) * q
+
         @pl.when(inner == 0)
         def _():
             for h in range(2):
                 at = slice(h * bit, (h + 1) * bit)
                 owner_came(q, 2, h).wait_recv()
-                back_out[q, 0, at] = mix(relay_ret[q, 2, at], ret_out[half + 2 * q, at], flags[q][0])
+                back_out[base, at] = mix(relay_ret[base + 2, at], ret_out[half + 2 * q, at], flags[q][0])
                 ret_merged(q, h).start()
 
     def frozen_block(i, carry):
@@ -634,38 +682,33 @@
 
     def base_block(i, carry):
         q = lax.rem(tensor_count - i, tensor_count)
-        acc[...] += nt_dot(cots[q], w_v[i])
+        acc[...] += nt_dot(cots[q].reshape(rows, out_block), w_v[i])
         return carry
 
     def rank_stage(g):
-        for s in groups[g]:
-            if s and s < half:
-                near_copy(s).wait_recv()
-            if s >= half and s % 2 == 1:
-                for h in range(2):
-                    slot_came(s, h).wait_recv()
-            if s >= half and s % 2 == 0:
-                @pl.when(inner == 0)
-                def _():
-                    for h in range(2):
-                        slot_came(s, h).wait_recv()
+        if g == 0:
+            near_came().wait_recv()
+        else:
+            slot_came(groups[g][1]).wait_recv()
+
+            @pl.when(inner == 0)
+            def _():
+                slot_came(groups[g][0]).wait_recv()
+
         for s in groups[g]:
             x = slot_in[lines(s), :block]
             c = slot_in[lines(s), block:]
             inner_s = nt_dot(x, down_ref[adapter_of[s]])
             back_s = nt_dot(c, up_ref[adapter_of[s]])
-            ranks[t, lines(s), :] = jnp.concatenate([inner_s, back_s], axis=1).astype(BF16)
+            ranks[lines(s), :] = jnp.concatenate([inner_s, back_s], axis=1).astype(BF16)
         for q in range(1, tensor_count):
             rank_copy(g, q).start()
 
     def use_stage(g):
-        for q in range(1, tensor_count):
-            rank_came(g, q).wait_recv()
-        for q in range(1, tensor_count):
-            rank_copy(g, q).wait_send()
-        total = ranks[0, rank_rows(g)].astype(F32)
-        for s in range(1, tensor_count):
-            total = total + ranks[s, rank_rows(g)].astype(F32)
+        ranks_came(g).wait_recv()
+        total = ranks[rank_rows(g)].astype(F32)
+        for s in range(tensor_count - 1):
+            total = total + ranks_in[s, rank_rows(g)].astype(F32)
         for m, s in enumerate(groups[g]):
             part = total[m * length:(m + 1) * length]
             mid = part[:, :rank].astype(BF16)
@@ -693,32 +736,49 @@
     lax.fori_loop(middle, tensor_count, frozen_block, 0)
     for q in range(1, tensor_count):
         part_copy(q).start()
-    acc[...] = nt_dot(cot_ref[...], w_v[0])
-    relay(far, 0)
-    for q in range(1, tensor_count):
-        cot_copy(q).wait_recv()
+    acc[...] = nt_dot(cot_ref[...].reshape(rows, out_block), w_v[0])
+    relay(close, 0)
+    cots_came().wait_recv()
     lax.fori_loop(1, middle, base_block, 0)
     down_copy.wait()
     up_copy.wait()
-    relay(far, 1)
+    onward(0)
+
+    relay(close, 1)
+
+    @pl.when(inner == 1)
+    def _():
+        near_copy(3).start()
+
     lax.fori_loop(middle, tensor_count, base_block, 0)
-    relay(far, 2)
-    relay(close, 0)
-    rank_stage(2)
-    relay(close, 1)
-    rank_stage(0)
-    use_stage(2)
+    onward(1)
     relay(close, 2)
-    use_stage(0)
-    merge_out(far)
-    hand_back(far, 0)
-    hand_back(far, 1)
-    hand_back(far, 2)
+    onward(2)
+    relay(far, 0)
     rank_stage(1)
     use_stage(1)
+    relay(far, 1)
+    rank_stage(0)
     merge_out(close)
-    for k in (3, 2, 1):
-        ret_near(k).start()
+    relay(far, 2)
+    use_stage(0)
+
+    @pl.when(inner == 1)
+    def _():
+        ret_near(3).start()
+
+    ret_near(2).start()
+    hand_back(close, 2)
+    hand_back(close, 1)
+    rank_stage(2)
+    hand_back(close, 0)
+    use_stage(2)
+    merge_out(far)
+    ret_near(1).start()
+
+    @pl.when(inner == 0)
+    def _():
+        ret_near(3).start()
 
     x_all = slot_in[:, :block]
     c_all = slot_in[:, block:]
@@ -729,50 +789,30 @@
             adapter_scale / jnp.maximum(jnp.full((1, out_block), counts[a], F32), 1.0))
     gd_copy.start()
     gu_copy.start()
-    for i in range(half - 1):
-        hand_back(close, i)
-    for q in range(1, tensor_count):
-        part_copy(q).wait_recv()
+    for i in (2, 1, 0):
+        hand_back(far, i)
+    parts_came().wait_recv()
     backbone = parts[0].astype(F32)
     for q in range(1, tensor_count):
         backbone = backbone + part_in[q].astype(F32)
-    for k in range(1, half):
-        ret_near(k).wait_recv()
-    for i in range(half - 1):
-        for h in range(2):
-            back_came(i, h).wait_recv()
+    rets_came().wait_recv()
     for j in range(seqs):
         came = ret_in[table_ref[8 + j]]
         kvo_ref[lines(j), :] = (backbone[lines(j)] + came[:, block:].astype(F32)).astype(BF16)
         tg_ref[lines(j), :] = (acc[lines(j), :] + came[:, :block].astype(F32)).astype(BF16)
 
-    for k in range(1, half):
-        near_copy(k).wait_send()
-        ret_near(k).wait_send()
-    for h in range(2):
-        for i in range(half - 1):
-            cross_copy(i, h).wait_send()
-        for q in range(2):
-            ret_other(q, h).wait_send()
+    cots_came().wait_send()
+    parts_came().wait_send()
+    ranks_sent().wait_send()
 
     @pl.when(inner == 0)
     def _():
-        for q in range(2):
-            for h in range(2):
-                ret_same(q, h).wait_send()
-                ret_merged(q, h).wait_send()
+        sent(5 * half - 5).wait_send()
 
     @pl.when(inner == 1)
     def _():
-        for q in range(2):
-            for i in range(half - 1):
-                for h in range(2):
-                    fwd_copy(q, i, h).wait_send()
-                    back_copy(q, i, h).wait_send()
-
-    for q in range(1, tensor_count):
-        cot_copy(q).wait_send()
-        part_copy(q).wait_send()
+        sent(dp_count + 6 * half - 6).wait_send()
+
     gd_copy.wait()
     gu_copy.wait()
 
@@ -884,55 +924,52 @@
     return pl.pallas_call(
         functools.partial(relay_kernel, dp_count, tensor_count),
         out_shape=shapes_of(rows, block, out_block, resident, rank),
-        in_specs=[smem, smem, vmem, anywhere, anywhere, anywhere, vmem, vmem],
+        in_specs=[smem, smem] + [anywhere] * 5,
         out_specs=(vmem, vmem, anywhere, anywhere),
         scratch_shapes=[
             pltpu.VMEM(down.shape, BF16),
             pltpu.VMEM(up.shape, BF16),
             pltpu.VMEM(down.shape, F32),
             pltpu.VMEM(up.shape, F32),
+            pltpu.VMEM((seqs, length, block), BF16),
+            pltpu.VMEM((seqs, length, out_block), BF16),
             pltpu.VMEM((tensor_count, w.shape[0], out_block), BF16),
             slots(half - 1),
             slots(half - 1),
+            slots(half - 1),
             pltpu.VMEM((dp_count * length, wide), BF16),
-            slots(2, half - 1),
             slots(2, half - 2),
-            slots(dp_count),
+            slots(dp_count + 6 * half - 6),
             slots(dp_count - 1),
-            slots(2, half - 1),
-            slots(2, half - 1),
+            pltpu.VMEM((tensor_count, seqs, length, out_block), BF16),
             pltpu.VMEM((tensor_count, rows, out_block), BF16),
             pltpu.VMEM((tensor_count, rows, out_block), BF16),
-            pltpu.VMEM((tensor_count, rows, out_block), BF16),
-            pltpu.VMEM((tensor_count, dp_count * length, 2 * rank), BF16),
+            pltpu.VMEM((dp_count * length, 2 * rank), BF16),
+            pltpu.VMEM((tensor_count - 1, dp_count * length, 2 * rank), BF16),
             pltpu.VMEM((resident, dp_count * length, rank), BF16),
             pltpu.VMEM((resident, dp_count * length, rank), BF16),
             pltpu.VMEM((rows, block), F32),
             dma((tensor_count,)),
-            dma((4,)),
+            dma((6,)),
+            dma,
+            dma,
             dma((half,)),
-            dma((half,)),
-            dma((half, 2)),
+            dma((2, half - 1, 2)),
             dma((half - 1, 2)),
             dma((2, half - 1, 2)),
-            dma((2, half - 1, 2)),
-            dma((dp_count, 2)),
-            dma((dp_count - 1, 2)),
-            dma((2, half - 1, 2)),
-            dma((2, half - 1, 2)),
-            dma((tensor_count,)),
-            dma((tensor_count,)),
-            dma((tensor_count,)),
-            dma((tensor_count,)),
-            dma((3, tensor_count)),
-            dma((3, tensor_count)),
+            dma,
+            dma,
+            dma,
+            dma,
+            dma,
+            dma,
+            dma((3,)),
         ],
         compiler_params=pltpu.CompilerParams(
             collective_id=0, has_side_effects=True, vmem_limit_bytes=60 * 1024 * 1024
         ),
     )(
-        table, weights, tok.reshape(seqs, length, block), w, down, up, cot,
-        cot.reshape(seqs, length, out_block))
+        table, weights, tok.reshape(seqs, length, block), w, down, up, cot.reshape(seqs, length, out_block))
 
 
 def on_device(dp_count, tensor_count, tok, w, down, up, cot, seq_index, storage):
@@ -944,17 +981,18 @@
     dma = pltpu.SemaphoreType.DMA
     args = (tok, w, down, up, cot)
     if relay_fits(dp_count, seqs):
-        table, weights = pl.pallas_call(
+        table, weights, fits = pl.pallas_call(
             functools.partial(relay_routes, dp_count, seqs, resident),
             out_shape=(
                 jax.ShapeDtypeStruct((32,), jnp.int32),
                 jax.ShapeDtypeStruct((resident * dp_count + resident,), F32),
+                jax.ShapeDtypeStruct((1,), jnp.int32),
             ),
             in_specs=[smem, smem],
-            out_specs=(smem, smem),
+            out_specs=(smem,) * 3,
         )(seq_index, storage)
         results = lax.cond(
-            table[7] > 0,
+            fits.reshape(()) > 0,
             lambda: relayed(dp_count, tensor_count, table, weights, *args, seqs),
             lambda: direct(dp_count, tensor_count, *args, seq_index, storage),
         )

time: 62.7 us -> 61.4 us (0.979)
  the two profiles are of different devices: /device:TPU:8 before, /device:TPU:0 now
where the time goes in v3:
time: 61.4 us; the launch traced here: 61.3 us
  Pallas kernels  59.9 us (98%)
  between operations  1.29 us (2%)
    pallas_call x1, Pallas kernels, relayed(): pl.pallas_call(functools.partial(relay_kernel, dp_count, tensor_count), o...  56.8 us
    pallas_call x1, Pallas kernels, on_device(): pl.pallas_call(functools.partial(relay_routes, dp_count, seqs, resident),...  1.55 us
    pallas_call x1, Pallas kernels, on_device(): pl.pallas_call(functools.partial(finish, pieces), out_shape=tuple((jax.Sh...  1.54 us

profile of v3, /device:TPU:0, one launch (start us, length us, event | category | flops | bytes accessed | tf_op | source)
XLA Modules:
  0.0 61.3 jit_solution(1673420748746229123)
XLA Ops:
  0.6 1.6 %shard_map.102 = (s32[32]{0:T(128)S(1)}, f32[27]{0:T(128)S(1)}, s32[1]{0:T(128)}) custom-call(s32[32]{0:T(128)} %seq_ref.1, s32[24]{0:T(128)} %store_ref.1), custom_call_target="tpu_custom_call" | custom-call | tf_op jit(solution)/shard_map/pallas_call | solution.py:984
  2.8 56.9 %conditional.1 = ((bf16[128,512]{1,0:T(8,128)(2,1)S(1)}, bf16[128,2048]{1,0:T(8,128)(2,1)S(1)}, f32[3,64,2048]{2,1,0:T(8,128)S(1)}, f32[3,64,512]{2,1,0:T(8,128)S(1)})) conditional(s32[]{:T(128)} %bitcast.4, (s32[32]{0:T(128)}, s32[24]{0:T(128)}, bf16[128,2048]{1,0:T(8,128)(2,1)}, bf16[128,512]{1,0:T(8,128)(2,1)}, bf16[2048,2048]{1,0:T(8,128)(2,1)}, ...), branch_computations={%region_0.0_spmd, %region_1.0_spmd} | conditional | bytes 8 | solution.py:994
  2.9 56.8 %branch_1_fun.1 = (bf16[128,512]{1,0:T(8,128)(2,1)S(1)}, bf16[128,2048]{1,0:T(8,128)(2,1)S(1)}, f32[3,64,2048]{2,1,0:T(8,128)S(1)}, f32[3,64,512]{2,1,0:T(8,128)S(1)}) custom-call(s32[32]{0:T(128)S(1)} %get-tuple-element.37.table_ref, f32[27]{0:T(128)S(1)} %get-tuple-element.38.weight_ref, bf16[4,32,2048]{2,1,0:T(8,128)(2,1)} %bitcast.6, ...), custom_call_target="tpu_custom_call" | custom-call | tf_op jit(solution)/shard_map/cond/branch_1_fun/pallas_call | solution.py:924
  59.7 1.5 %shard_map.103 = (bf16[128,512]{1,0:T(8,128)(2,1)}, bf16[128,2048]{1,0:T(8,128)(2,1)}, f32[3,64,2048]{2,1,0:T(8,128)}, f32[3,64,512]{2,1,0:T(8,128)}) custom-call(bf16[128,512]{1,0:T(8,128)(2,1)S(1)} %get-tuple-element.58.refs_0_, bf16[128,2048]{1,0:T(8,128)(2,1)S(1)} %get-tuple-element.59.refs_1_, f32[3,64,2048]{2,1,0:T(8,128)S(1)} %get-tuple-element.60.refs_2_, ...), custom_call_target="tpu_custom_call" | custom-call | tf_op jit(solution)/shard_map/pallas_call | solution.py:1002

commit v4 on v3

--- a/solution.py
+++ b/solution.py
@@ -498,11 +498,10 @@
     def fwd_copy(q, m, h):
         s = half + 2 * q + (0 if m == 1 else 1)
         source = relay_out.at[q, m - 1, piece(h)] if m else relay_in.at[(half - 1) * q, piece(h)]
-        return over(source, slot_at(s, h), send_sem, slot_rsem.at[s - half], dp=peer[3 - m])
-
-    def slot_came(s):
-        at = slot_in.at[pl.ds(s * length, length)]
-        return over(at, at, send_sem, slot_rsem.at[s - half], dp=peer[1])
+        return over(source, slot_at(s, h), send_sem, slot_rsem.at[s - half, h], dp=peer[3 - m])
+
+    def slot_came(s, h):
+        return over(slot_at(s, h), slot_at(s, h), send_sem, slot_rsem.at[s - half, h], dp=peer[1])
 
     def ret_near(k):
         return over(ret_out.at[k], ret_in.at[k], send_sem, ret_rsem, dp=peer[k])
@@ -548,15 +547,26 @@
         at = part_in.at[pl.ds(1, tensor_count - 1)]
         return over(at, at, part_ssem, part_rsem, tensor=t_to(1))
 
-    def rank_rows(g):
-        return pl.ds(starts[g] * length, len(groups[g]) * length)
-
-    def rank_copy(g, q):
-        return over(ranks.at[rank_rows(g)], ranks_in.at[q - 1, rank_rows(g)], rank_ssem, rank_rsem.at[g], tensor=t_to(q))
-
-    def ranks_came(g):
-        at = ranks_in.at[:, rank_rows(g)]
-        return over(at, at, rank_ssem, rank_rsem.at[g], tensor=t_to(1))
+    def spans(g, h):
+        size = length if g == 0 else bit
+        return [(s, slice(s * length + h * size, s * length + (h + 1) * size)) for s in groups[g]]
+
+    def rank_at(g, h):
+        return 2 * starts[g] * bit + h * len(groups[g]) * bit
+
+    def rank_rows(g, h):
+        return pl.ds(rank_at(g, h), len(groups[g]) * (length if g == 0 else bit))
+
+    def rank_sem(g, h):
+        return rank_rsem.at[2 * g - 1 + h if g else 0]
+
+    def rank_copy(g, h, q):
+        return over(ranks.at[rank_rows(g, h)], ranks_in.at[q - 1, rank_rows(g, h)],
+                    rank_ssem, rank_sem(g, h), tensor=t_to(q))
+
+    def ranks_came(g, h):
+        at = ranks_in.at[:, rank_rows(g, h)]
+        return over(at, at, rank_ssem, rank_sem(g, h), tensor=t_to(1))
 
     def ranks_sent():
         return over(ranks_in, ranks_in, rank_ssem, rank_rsem.at[0], tensor=t_to(1))
@@ -685,51 +695,55 @@
         acc[...] += nt_dot(cots[q].reshape(rows, out_block), w_v[i])
         return carry
 
-    def rank_stage(g):
+    def rank_stage(g, h):
         if g == 0:
             near_came().wait_recv()
         else:
-            slot_came(groups[g][1]).wait_recv()
+            slot_came(groups[g][1], h).wait_recv()
 
             @pl.when(inner == 0)
             def _():
-                slot_came(groups[g][0]).wait_recv()
-
-        for s in groups[g]:
-            x = slot_in[lines(s), :block]
-            c = slot_in[lines(s), block:]
+                slot_came(groups[g][0], h).wait_recv()
+
+        base = rank_at(g, h)
+        for s, at in spans(g, h):
+            x = slot_in[at, :block]
+            c = slot_in[at, block:]
             inner_s = nt_dot(x, down_ref[adapter_of[s]])
             back_s = nt_dot(c, up_ref[adapter_of[s]])
-            ranks[lines(s), :] = jnp.concatenate([inner_s, back_s], axis=1).astype(BF16)
+            size = at.stop - at.start
+            ranks[base:base + size, :] = jnp.concatenate([inner_s, back_s], axis=1).astype(BF16)
+            base += size
         for q in range(1, tensor_count):
-            rank_copy(g, q).start()
-
-    def use_stage(g):
-        ranks_came(g).wait_recv()
-        total = ranks[rank_rows(g)].astype(F32)
+            rank_copy(g, h, q).start()
+
+    def use_stage(g, h):
+        ranks_came(g, h).wait_recv()
+        total = ranks[rank_rows(g, h)].astype(F32)
         for s in range(tensor_count - 1):
-            total = total + ranks_in[s, rank_rows(g)].astype(F32)
-        for m, s in enumerate(groups[g]):
-            part = total[m * length:(m + 1) * length]
+            total = total + ranks_in[s, rank_rows(g, h)].astype(F32)
+        base = 0
+        for s, at in spans(g, h):
+            size = at.stop - at.start
+            part = total[base:base + size]
+            base += size
             mid = part[:, :rank].astype(BF16)
             back = part[:, rank:].astype(BF16)
             target = ret_out if s else ret_in
-            target[s, :, :block] = (adapter_scale * jnp.dot(
+            to = slice(at.start - s * length, at.stop - s * length)
+            target[s, to, :block] = (adapter_scale * jnp.dot(
                 back, down_ref[adapter_of[s]], preferred_element_type=F32)).astype(BF16)
-            target[s, :, block:] = (adapter_scale * jnp.dot(
+            target[s, to, block:] = (adapter_scale * jnp.dot(
                 mid, up_ref[adapter_of[s]], preferred_element_type=F32)).astype(BF16)
             for a in range(resident):
-                back_m[a, lines(s), :] = (back.astype(F32) * weights[a][s]).astype(BF16)
-                inner_m[a, lines(s), :] = (mid.astype(F32) * weights[a][s]).astype(BF16)
+                back_m[a, at, :] = (back.astype(F32) * weights[a][s]).astype(BF16)
+                inner_m[a, at, :] = (mid.astype(F32) * weights[a][s]).astype(BF16)
         if g:
-            q = g - 1
-            for h in range(2):
-                ret_other(q, h).start()
+            ret_other(g - 1, h).start()
 
             @pl.when(inner == 0)
             def _():
-                for h in range(2):
-                    ret_same(q, h).start()
+                ret_same(g - 1, h).start()
 
     middle = max(1, tensor_count // 2)
     lax.fori_loop(0, middle, frozen_block, 0)
@@ -753,15 +767,17 @@
     lax.fori_loop(middle, tensor_count, base_block, 0)
     onward(1)
     relay(close, 2)
+    rank_stage(1, 0)
     onward(2)
     relay(far, 0)
-    rank_stage(1)
-    use_stage(1)
+    rank_stage(1, 1)
+    use_stage(1, 0)
+    use_stage(1, 1)
     relay(far, 1)
-    rank_stage(0)
+    rank_stage(0, 0)
     merge_out(close)
     relay(far, 2)
-    use_stage(0)
+    use_stage(0, 0)
 
     @pl.when(inner == 1)
     def _():
@@ -770,14 +786,16 @@
     ret_near(2).start()
     hand_back(close, 2)
     hand_back(close, 1)
-    rank_stage(2)
+    rank_stage(2, 0)
+    rank_stage(2, 1)
     hand_back(close, 0)
-    use_stage(2)
+    use_stage(2, 0)
+    use_stage(2, 1)
     merge_out(far)
-    ret_near(1).start()
 
     @pl.when(inner == 0)
     def _():
+        ret_near(1).start()
         ret_near(3).start()
 
     x_all = slot_in[:, :block]
@@ -789,8 +807,14 @@
             adapter_scale / jnp.maximum(jnp.full((1, out_block), counts[a], F32), 1.0))
     gd_copy.start()
     gu_copy.start()
-    for i in (2, 1, 0):
-        hand_back(far, i)
+    hand_back(far, 2)
+
+    @pl.when(inner == 1)
+    def _():
+        ret_near(1).start()
+
+    hand_back(far, 1)
+    hand_back(far, 0)
     parts_came().wait_recv()
     backbone = parts[0].astype(F32)
     for q in range(1, tensor_count):
@@ -953,7 +977,7 @@
             dma((6,)),
             dma,
             dma,
-            dma((half,)),
+            dma((half, 2)),
             dma((2, half - 1, 2)),
             dma((half - 1, 2)),
             dma((2, half - 1, 2)),
@@ -963,7 +987,7 @@
             dma,
             dma,
             dma,
-            dma((3,)),
+            dma((5,)),
         ],
         compiler_params=pltpu.CompilerParams(
             collective_id=0, has_side_effects=True, vmem_limit_bytes=60 * 1024 * 1024

time: 61.4 us -> 59.8 us (0.974)
  Pallas kernels: 59.9 us -> 58.3 us
    pallas_call x1, Pallas kernels: 56.8 us -> 55.2 us  [relayed(): pl.pallas_call(functools.partial(relay_kernel, dp_count, tensor_count), o...]
where the time goes in v4:
time: 59.8 us; the launch traced here: 59.6 us
  Pallas kernels  58.3 us (97%)
  between operations  1.29 us (2%)
    pallas_call x1, Pallas kernels, relayed(): pl.pallas_call(functools.partial(relay_kernel, dp_count, tensor_count), o...  55.2 us
    pallas_call x1, Pallas kernels, on_device(): pl.pallas_call(functools.partial(relay_routes, dp_count, seqs, resident),...  1.55 us
    pallas_call x1, Pallas kernels, on_device(): pl.pallas_call(functools.partial(finish, pieces), out_shape=tuple((jax.Sh...  1.54 us

profile of v4, /device:TPU:0, one launch (start us, length us, event | category | flops | bytes accessed | tf_op | source)
XLA Modules:
  0.0 59.6 jit_solution(19841053268142896)
XLA Ops:
  0.6 1.6 %shard_map.102 = (s32[32]{0:T(128)S(1)}, f32[27]{0:T(128)S(1)}, s32[1]{0:T(128)}) custom-call(s32[32]{0:T(128)} %seq_ref.1, s32[24]{0:T(128)} %store_ref.1), custom_call_target="tpu_custom_call" | custom-call | tf_op jit(solution)/shard_map/pallas_call | solution.py:1008
  2.8 55.2 %conditional.1 = ((bf16[128,512]{1,0:T(8,128)(2,1)S(1)}, bf16[128,2048]{1,0:T(8,128)(2,1)S(1)}, f32[3,64,2048]{2,1,0:T(8,128)S(1)}, f32[3,64,512]{2,1,0:T(8,128)S(1)})) conditional(s32[]{:T(128)} %bitcast.4, (s32[32]{0:T(128)}, s32[24]{0:T(128)}, bf16[128,2048]{1,0:T(8,128)(2,1)}, bf16[128,512]{1,0:T(8,128)(2,1)}, bf16[2048,2048]{1,0:T(8,128)(2,1)}, ...), branch_computations={%region_0.0_spmd, %region_1.0_spmd} | conditional | bytes 8 | solution.py:1018
  2.9 55.2 %branch_1_fun.1 = (bf16[128,512]{1,0:T(8,128)(2,1)S(1)}, bf16[128,2048]{1,0:T(8,128)(2,1)S(1)}, f32[3,64,2048]{2,1,0:T(8,128)S(1)}, f32[3,64,512]{2,1,0:T(8,128)S(1)}) custom-call(s32[32]{0:T(128)S(1)} %get-tuple-element.37.table_ref, f32[27]{0:T(128)S(1)} %get-tuple-element.38.weight_ref, bf16[4,32,2048]{2,1,0:T(8,128)(2,1)} %bitcast.6, ...), custom_call_target="tpu_custom_call" | custom-call | tf_op jit(solution)/shard_map/cond/branch_1_fun/pallas_call | solution.py:948
  58.0 1.5 %shard_map.103 = (bf16[128,512]{1,0:T(8,128)(2,1)}, bf16[128,2048]{1,0:T(8,128)(2,1)}, f32[3,64,2048]{2,1,0:T(8,128)}, f32[3,64,512]{2,1,0:T(8,128)}) custom-call(bf16[128,512]{1,0:T(8,128)(2,1)S(1)} %get-tuple-element.58.refs_0_, bf16[128,2048]{1,0:T(8,128)(2,1)S(1)} %get-tuple-element.59.refs_1_, f32[3,64,2048]{2,1,0:T(8,128)S(1)} %get-tuple-element.60.refs_2_, ...), custom_call_target="tpu_custom_call" | custom-call | tf_op jit(solution)/shard_map/pallas_call | solution.py:1026

commit v5 on v4

--- a/solution.py
+++ b/solution.py
@@ -765,8 +765,8 @@
         near_copy(3).start()
 
     lax.fori_loop(middle, tensor_count, base_block, 0)
+    relay(close, 2)
     onward(1)
-    relay(close, 2)
     rank_stage(1, 0)
     onward(2)
     relay(far, 0)

time: 59.8 us -> 58.8 us (0.983)
  Pallas kernels: 58.3 us -> 57.3 us
    pallas_call x1, Pallas kernels: 55.2 us -> 54.2 us  [relayed(): pl.pallas_call(functools.partial(relay_kernel, dp_count, tensor_count), o...]
where the time goes in v5:
time: 58.8 us; the launch traced here: 58.6 us
  Pallas kernels  57.3 us (97%)
  between operations  1.29 us (2%)
    pallas_call x1, Pallas kernels, relayed(): pl.pallas_call(functools.partial(relay_kernel, dp_count, tensor_count), o...  54.2 us
    pallas_call x1, Pallas kernels, on_device(): pl.pallas_call(functools.partial(relay_routes, dp_count, seqs, resident),...  1.55 us
    pallas_call x1, Pallas kernels, on_device(): pl.pallas_call(functools.partial(finish, pieces), out_shape=tuple((jax.Sh...  1.54 us

profile of v5, /device:TPU:0, one launch (start us, length us, event | category | flops | bytes accessed | tf_op | source)
XLA Modules:
  0.0 58.6 jit_solution(89310050491587009)
XLA Ops:
  0.6 1.6 %shard_map.102 = (s32[32]{0:T(128)S(1)}, f32[27]{0:T(128)S(1)}, s32[1]{0:T(128)}) custom-call(s32[32]{0:T(128)} %seq_ref.1, s32[24]{0:T(128)} %store_ref.1), custom_call_target="tpu_custom_call" | custom-call | tf_op jit(solution)/shard_map/pallas_call | solution.py:1008
  2.8 54.2 %conditional.1 = ((bf16[128,512]{1,0:T(8,128)(2,1)S(1)}, bf16[128,2048]{1,0:T(8,128)(2,1)S(1)}, f32[3,64,2048]{2,1,0:T(8,128)S(1)}, f32[3,64,512]{2,1,0:T(8,128)S(1)})) conditional(s32[]{:T(128)} %bitcast.4, (s32[32]{0:T(128)}, s32[24]{0:T(128)}, bf16[128,2048]{1,0:T(8,128)(2,1)}, bf16[128,512]{1,0:T(8,128)(2,1)}, bf16[2048,2048]{1,0:T(8,128)(2,1)}, ...), branch_computations={%region_0.0_spmd, %region_1.0_spmd} | conditional | bytes 8 | solution.py:1018
  2.9 54.2 %branch_1_fun.1 = (bf16[128,512]{1,0:T(8,128)(2,1)S(1)}, bf16[128,2048]{1,0:T(8,128)(2,1)S(1)}, f32[3,64,2048]{2,1,0:T(8,128)S(1)}, f32[3,64,512]{2,1,0:T(8,128)S(1)}) custom-call(s32[32]{0:T(128)S(1)} %get-tuple-element.37.table_ref, f32[27]{0:T(128)S(1)} %get-tuple-element.38.weight_ref, bf16[4,32,2048]{2,1,0:T(8,128)(2,1)} %bitcast.6, ...), custom_call_target="tpu_custom_call" | custom-call | tf_op jit(solution)/shard_map/cond/branch_1_fun/pallas_call | solution.py:948
  57.1 1.5 %shard_map.103 = (bf16[128,512]{1,0:T(8,128)(2,1)}, bf16[128,2048]{1,0:T(8,128)(2,1)}, f32[3,64,2048]{2,1,0:T(8,128)}, f32[3,64,512]{2,1,0:T(8,128)}) custom-call(bf16[128,512]{1,0:T(8,128)(2,1)S(1)} %get-tuple-element.58.refs_0_, bf16[128,2048]{1,0:T(8,128)(2,1)S(1)} %get-tuple-element.59.refs_1_, f32[3,64,2048]{2,1,0:T(8,128)S(1)} %get-tuple-element.60.refs_2_, ...), custom_call_target="tpu_custom_call" | custom-call | tf_op jit(solution)/shard_map/pallas_call | solution.py:1026

commit v6 on v5

--- a/solution.py
+++ b/solution.py
@@ -578,8 +578,6 @@
 
     tok_copy = pltpu.make_async_copy(tok_hbm, tok_ref, local_sem.at[4])
     seed_copy = pltpu.make_async_copy(cot_hbm, cot_ref, local_sem.at[5])
-    tok_copy.start()
-    seed_copy.start()
 
     barrier = pltpu.get_barrier_semaphore()
     for k in range(1, half + 1):
@@ -591,6 +589,8 @@
 
     for q in range(1, tensor_count):
         pl.semaphore_signal(barrier, inc=1, device_id={"tensor": t_to(q)}, device_id_type=MESH)
+    tok_copy.start()
+    seed_copy.start()
     for i in range(tensor_count):
         w_copy(i).start()
     down_copy.start()
@@ -768,9 +768,9 @@
     relay(close, 2)
     onward(1)
     rank_stage(1, 0)
+    rank_stage(1, 1)
     onward(2)
     relay(far, 0)
-    rank_stage(1, 1)
     use_stage(1, 0)
     use_stage(1, 1)
     relay(far, 1)
@@ -779,13 +779,14 @@
     relay(far, 2)
     use_stage(0, 0)
 
+    hand_back(close, 2)
+    hand_back(close, 1)
+
     @pl.when(inner == 1)
     def _():
         ret_near(3).start()
 
     ret_near(2).start()
-    hand_back(close, 2)
-    hand_back(close, 1)
     rank_stage(2, 0)
     rank_stage(2, 1)
     hand_back(close, 0)

time: 58.8 us -> 58.8 us (level)
  no operation moved by 1% of the time
where the time goes in v6:
time: 58.8 us; the launch traced here: 58.6 us
  Pallas kernels  57.3 us (97%)
  between operations  1.29 us (2%)
    pallas_call x1, Pallas kernels, relayed(): pl.pallas_call(functools.partial(relay_kernel, dp_count, tensor_count), o...  54.2 us
    pallas_call x1, Pallas kernels, on_device(): pl.pallas_call(functools.partial(relay_routes, dp_count, seqs, resident),...  1.55 us
    pallas_call x1, Pallas kernels, on_device(): pl.pallas_call(functools.partial(finish, pieces), out_shape=tuple((jax.Sh...  1.54 us

profile of v6, /device:TPU:0, one launch (start us, length us, event | category | flops | bytes accessed | tf_op | source)
XLA Modules:
  0.0 58.6 jit_solution(14226511720486629416)
XLA Ops:
  0.6 1.6 %shard_map.102 = (s32[32]{0:T(128)S(1)}, f32[27]{0:T(128)S(1)}, s32[1]{0:T(128)}) custom-call(s32[32]{0:T(128)} %seq_ref.1, s32[24]{0:T(128)} %store_ref.1), custom_call_target="tpu_custom_call" | custom-call | tf_op jit(solution)/shard_map/pallas_call | solution.py:1009
  2.8 54.3 %conditional.1 = ((bf16[128,512]{1,0:T(8,128)(2,1)S(1)}, bf16[128,2048]{1,0:T(8,128)(2,1)S(1)}, f32[3,64,2048]{2,1,0:T(8,128)S(1)}, f32[3,64,512]{2,1,0:T(8,128)S(1)})) conditional(s32[]{:T(128)} %bitcast.4, (s32[32]{0:T(128)}, s32[24]{0:T(128)}, bf16[128,2048]{1,0:T(8,128)(2,1)}, bf16[128,512]{1,0:T(8,128)(2,1)}, bf16[2048,2048]{1,0:T(8,128)(2,1)}, ...), branch_computations={%region_0.0_spmd, %region_1.0_spmd} | conditional | bytes 8 | solution.py:1019
  2.9 54.2 %branch_1_fun.1 = (bf16[128,512]{1,0:T(8,128)(2,1)S(1)}, bf16[128,2048]{1,0:T(8,128)(2,1)S(1)}, f32[3,64,2048]{2,1,0:T(8,128)S(1)}, f32[3,64,512]{2,1,0:T(8,128)S(1)}) custom-call(s32[32]{0:T(128)S(1)} %get-tuple-element.37.table_ref, f32[27]{0:T(128)S(1)} %get-tuple-element.38.weight_ref, bf16[4,32,2048]{2,1,0:T(8,128)(2,1)} %bitcast.6, ...), custom_call_target="tpu_custom_call" | custom-call | tf_op jit(solution)/shard_map/cond/branch_1_fun/pallas_call | solution.py:949
  57.1 1.5 %shard_map.103 = (bf16[128,512]{1,0:T(8,128)(2,1)}, bf16[128,2048]{1,0:T(8,128)(2,1)}, f32[3,64,2048]{2,1,0:T(8,128)}, f32[3,64,512]{2,1,0:T(8,128)}) custom-call(bf16[128,512]{1,0:T(8,128)(2,1)S(1)} %get-tuple-element.58.refs_0_, bf16[128,2048]{1,0:T(8,128)(2,1)S(1)} %get-tuple-element.59.refs_1_, f32[3,64,2048]{2,1,0:T(8,128)S(1)} %get-tuple-element.60.refs_2_, ...), custom_call_target="tpu_custom_call" | custom-call | tf_op jit(solution)/shard_map/pallas_call | solution.py:1027
